TPU v7x, 1024 devices: a whole 8x8x8 slice. The times are simulated.
1024 devices in a mesh: dp: 64 (over x, y), tensor: 8 (over z_lo, core), section: 2 (over z_hi).
Axes of the slice: x: 8, y: 8, z: 8 (z_hi: 2, z_lo: 4; z = z_hi * 4 + z_lo), core: 2. Of those that a mesh axis runs over, the one named last changes fastest.
Arguments:
- w_value: bfloat16 [8192, 1024], P(('dp', 'section'), 'tensor'), may hold values from -0.0625 to 0.0625
- hidden_new: bfloat16 [384, 4, 8192], P(('dp', 'section')), may hold values from -6 to 6
- query: bfloat16 [384, 4, 8192], P(('dp', 'section'), None, 'tensor'), may hold values from -240 to 240
- key_new: bfloat16 [384, 4, 1024], P(('dp', 'section'), None, 'tensor'), may hold values from -6 to 6
- key_cache: bfloat16 [384, 2048, 1024], P(('dp', 'section'), None, 'tensor'), may hold values from -6 to 6
- value_cache: bfloat16 [384, 2048, 1024], P(('dp', 'section'), None, 'tensor'), may hold values from -6 to 6
- cache_len: int32 [384], P(('dp', 'section')), may hold values from 512 to 2048, as said below
- sampled_rows: bfloat16 [16384, 8192], P(('dp', 'section')), may hold values from -6 to 6
- mb_map: int32 [128, 128], P(('dp', 'section')), may hold values from 0 to 127, each once within a row
- value_target: bfloat16 [16384, 1024], P(('dp', 'section'), 'tensor'), may hold values from -6 to 6
Outputs:
- attn_out: bfloat16 [384, 4, 8192], P(('dp', 'section'), None, 'tensor')
- grad_value: float32 [8192, 1024], P(('dp', 'section'), 'tensor')
Inputs may be any that keep to these rules, and one draw needn't show every extreme that they name: `cache_len`: each prompt has at least 512 live positions; some prompt has exactly 2048.
All inputs are finite; a program needn't handle non-finite values.
Results may differ from a plain program's by a relative error of at most 0.0049.
Values may be sent and summed in bfloat16 or wider, within the bound.
No kernel may reach another device: no remote copies, remote signals or barrier semaphores. Data moves between devices by JAX's collectives and lax.ppermute only.
A program may use at most 64 MiB of HBM per device.

v0:
```python
import jax
import jax.numpy as jnp
from jax import lax
from jax.sharding import Mesh
from jax.sharding import PartitionSpec as P

HD = 128
QPK = 8
NEW = 4
DP = ("dp_0", "dp_1")
DP_SECTION = ("dp_0", "dp_1", "section")


def split_up(shard, dim, peers):
    before, after = (shard.shape[:dim], shard.shape[dim + 1 :])
    return jnp.moveaxis(shard.reshape(*before, peers, -1, *after), dim, 0)


def laid_out(blocks, dim):
    blocks = jnp.moveaxis(blocks, 0, dim)
    lengths = blocks.shape
    return blocks.reshape(*lengths[:dim], lengths[dim] * lengths[dim + 1], *lengths[dim + 2 :])


def turned_blocks(blocks, axes, sequence):
    inside = blocks.shape[1:]
    out = blocks.reshape(*(lax.axis_size(a) for a in axes), *inside)
    for k in sequence:
        out = lax.all_to_all(out, axes[k], k, k, tiled=True)
    return out.reshape(-1, *inside)


def stepwise_exchange(shard, axes, sequence, split_dim, concat_dim):
    blocks = split_up(shard, split_dim, lax.axis_size(axes))
    return laid_out(turned_blocks(blocks, axes, sequence), concat_dim)


def gather_in_order(shard, axes, sequence):
    blocks = shard[None]
    for k in sequence:
        blocks = lax.all_gather(blocks, axes[k], axis=0, tiled=True)
    current = [lax.axis_size(axes[k]) for k in reversed(sequence)]
    blocks = blocks.reshape(*current, *shard.shape)
    turned = sorted(range(len(sequence)), key=lambda place: sequence[len(sequence) - 1 - place])
    return blocks.transpose(*turned, *range(len(sequence), blocks.ndim)).reshape(-1, *shard.shape)


def whole_of(shard, axes, sequence, dim):
    return laid_out(gather_in_order(shard, axes, sequence), dim)


def own_rows(running, axes):
    for axis in axes:
        running = lax.psum_scatter(running, axis, scatter_dimension=0, tiled=True)
    return running


def per_device(
    w_value,
    hidden_new,
    query,
    key_new,
    key_cache,
    value_cache,
    cache_len,
    sampled_rows,
    mb_map,
    value_target,
):
    replicas = lax.axis_size(DP)
    row_count = sampled_rows.shape[0]
    per_peer = row_count // replicas
    order = mb_map[0]
    pieces = value_target.reshape(replicas, per_peer, value_target.shape[1])
    returned = stepwise_exchange(pieces, DP, (0, 1), 0, 0).reshape(row_count, value_target.shape[1])
    train_target = jnp.zeros_like(returned).at[order].set(returned)
    prompts = hidden_new.shape[0]
    width_local = w_value.shape[1]
    new_rows = hidden_new.reshape(prompts * NEW, hidden_new.shape[2])
    piece = whole_of(w_value, DP_SECTION, (2, 0, 1), 0)
    v_new_full = jnp.dot(new_rows, piece, preferred_element_type=jnp.float32)
    v_train = jnp.dot(sampled_rows, piece, preferred_element_type=jnp.float32)
    residual_value = (v_train - train_target.astype(jnp.float32)).astype(jnp.bfloat16)
    grad_value = (
        own_rows(
            lax.dot_general(
                sampled_rows,
                residual_value,
                (((0,), (0,)), ((), ())),
                preferred_element_type=jnp.float32,
            ),
            DP_SECTION,
        )
        / row_count
    )
    heads_local = width_local // HD
    cache_size = key_cache.shape[1]
    scale = 1.0 / jnp.sqrt(jnp.float32(HD))
    v_new = v_new_full.astype(jnp.bfloat16).reshape(prompts, NEW, heads_local, HD)
    query_h = query.reshape(prompts, NEW, heads_local, QPK, HD)
    kc_heads = key_cache.reshape(prompts, cache_size, heads_local, HD)
    vc_heads = value_cache.reshape(prompts, cache_size, heads_local, HD)
    kn_heads = key_new.reshape(prompts, NEW, heads_local, HD)
    score_cache = (
        jnp.einsum("ptgqd,pjgd->pgtqj", query_h, kc_heads, preferred_element_type=jnp.float32)
        * scale
    )
    score_new = (
        jnp.einsum("ptgqd,pugd->pgtqu", query_h, kn_heads, preferred_element_type=jnp.float32)
        * scale
    )
    live_cache = (jnp.arange(cache_size)[None, :] < cache_len[:, None])[:, None, None, None, :]
    live_new = (jnp.arange(NEW)[None, :] <= jnp.arange(NEW)[:, None])[None, None, :, None, :]
    score_cache = jnp.where(live_cache, score_cache, -1e30)
    score_new = jnp.where(live_new, score_new, -1e30)
    peak = jnp.maximum(jnp.max(score_cache, axis=-1), jnp.max(score_new, axis=-1))[..., None]
    exp_cache = jnp.where(live_cache, jnp.exp(score_cache - peak), 0.0)
    exp_new = jnp.where(live_new, jnp.exp(score_new - peak), 0.0)
    total = jnp.sum(exp_cache, axis=-1, keepdims=True) + jnp.sum(exp_new, axis=-1, keepdims=True)
    prob_cache = (exp_cache / total).astype(jnp.bfloat16)
    prob_new = (exp_new / total).astype(jnp.bfloat16)
    mixed = jnp.einsum(
        "pgtqj,pjgd->ptgqd", prob_cache, vc_heads, preferred_element_type=jnp.float32
    )
    mixed = mixed + jnp.einsum(
        "pgtqu,pugd->ptgqd", prob_new, v_new, preferred_element_type=jnp.float32
    )
    attn_out = mixed.reshape(prompts, NEW, heads_local * QPK * HD).astype(jnp.bfloat16)
    return (attn_out, grad_value)


def solution(mesh):
    torus = Mesh(
        mesh.devices.reshape(8, 8, mesh.shape["tensor"], mesh.shape["section"]),
        ("dp_0", "dp_1", "tensor", "section"),
    )
    return jax.shard_map(
        per_device,
        mesh=torus,
        in_specs=(
            P(DP_SECTION, "tensor"),
            P(DP_SECTION, None, None),
            P(DP_SECTION, None, "tensor"),
            P(DP_SECTION, None, "tensor"),
            P(DP_SECTION, None, "tensor"),
            P(DP_SECTION, None, "tensor"),
            P(DP_SECTION),
            P(DP_SECTION, None),
            P(DP_SECTION, None),
            P(DP_SECTION, "tensor"),
        ),
        out_specs=(P(DP_SECTION, None, "tensor"), P(DP_SECTION, "tensor")),
        check_vma=False,
    )
```

profile of v0, /device:TPU:1, one launch (start us, length us, event | category | flops | bytes accessed | tf_op | source)
XLA Modules:
  0.0 251.1 jit_solution(8698231160998664916)
XLA Ops:
  7.2 0.0 copy-start
  7.2 0.0 all-gather.3.cloned.1.call-start
  7.2 15.4 %all-gather = bf16[128,128]{1,0:T(8,128)(2,1)S(1)} all-gather(bf16[64,128]{1,0:T(8,128)(2,1)} %param.10), channel_id=2, replica_groups=mesh['dp_0'=8,'dp_1'=8,'tensor'=8,'section'=2] {'section'}, dimensions={0}, use_global_device_ids=true | all-gather | bytes 49152 | tf_op jit(solution)/shard_map/all_gather | solution.py:41
  22.6 21.7 %all_gather.10 = bf16[16,64,128]{2,1,0:T(8,128)(2,1)} all-gather(bf16[2,64,128]{2,1,0:T(8,128)(2,1)S(1)} %bitcast.71), channel_id=1, replica_groups=mesh['dp_0'=8,'dp_1'=8,'tensor'=8,'section'=2] {'dp_0'}, dimensions={0}, use_global_device_ids=true | all-gather | bytes 294912 | tf_op jit(solution)/shard_map/all_gather | solution.py:41
  44.3 0.0 all-gather.3.cloned.1.call-update
  44.3 12.4 %all_to_all.10 = bf16[8,8,1,2,128]{4,3,1,2,0:T(2,128)(2,1)S(1)} all-to-all(bf16[8,8,1,2,128]{4,3,1,2,0:T(2,128)(2,1)} %bitcast.72), channel_id=1, replica_groups=mesh['dp_0'=8,'dp_1'=8,'tensor'=8,'section'=2] {'dp_0'}, dimensions={0} | all-to-all | bytes 65536 | tf_op jit(solution)/shard_map/all_to_all | solution.py:29
  56.7 0.6 copy.17
  57.3 7.5 %all-to-all-start.1 = ((bf16[8,8,1,2,128]{4,3,0,2,1:T(2,128)(2,1)}), bf16[8,8,1,2,128]{4,3,0,2,1:T(2,128)(2,1)S(1)}, u32[]{:S(2)}, u32[]{:S(2)}) async-start(bf16[8,8,1,2,128]{4,3,0,2,1:T(2,128)(2,1)} %copy.17), calls=%async_computation.1 | async-start | bytes 65536 | tf_op jit(solution)/shard_map/all_to_all | solution.py:29
  64.8 0.0 reduce-scatter.6.cloned.1.call-start
  64.9 0.7 fusion.34
  65.5 6.2 %all-to-all-done.1 = bf16[8,8,1,2,128]{4,3,0,2,1:T(2,128)(2,1)S(1)} async-done(((bf16[8,8,1,2,128]{4,3,0,2,1:T(2,128)(2,1)}), bf16[8,8,1,2,128]{4,3,0,2,1:T(2,128)(2,1)S(1)}, u32[]{:S(2)}, u32[]{:S(2)}) %all-to-all-start.1) | async-done | bytes 32800 | tf_op jit(solution)/shard_map/all_to_all | solution.py:29
  71.7 0.9 scatter_custom_fusion
  72.6 24.5 %all-gather.3.cloned.1.call-done = bf16[128,64,128]{2,1,0:T(8,128)(2,1)} async-done(((bf16[16,64,128]{2,1,0:T(8,128)(2,1)}), bf16[128,64,128]{2,1,0:T(8,128)(2,1)}) %all-gather.3.cloned.1.call-update) | async-done | bytes 2097168 | tf_op jit(solution)/shard_map/all_gather | solution.py:41
  97.1 3.2 %copy.16 = bf16[8,8,2,64,128]{4,3,2,1,0:T(8,128)(2,1)} copy(bf16[8,8,2,64,128]{4,3,2,0,1:T(8,128)(2,1)} %bitcast.70) | data formatting | bytes 4194304 | tf_op jit(solution)/shard_map/transpose | solution.py:45
  100.4 0.0 copy-done
  100.4 4.9 %convolution_bitcast_fusion = f32[8192,128]{0,1:T(8,128)} fusion(bf16[128,8192]{1,0:T(8,128)(2,1)S(1)} %copy-done, bf16[8192,128]{1,0:T(8,128)(2,1)} %bitcast.68, bf16[128,128]{1,0:T(8,128)(2,1)S(1)} %scatter_custom_fusion), kind=kOutput, calls=%fused_computation.1 | convolution fusion | flops 536920064 | bytes 8421376 | tf_op jit(solution)/shard_map/dot_general | solution.py:86
  105.3 0.0 copy-start.3
  105.3 0.0 copy-start.2
  105.3 0.0 copy-start.5
  105.3 0.0 copy-start.4
  105.3 0.0 reduce-scatter.6.cloned.1.call-update
  105.3 0.0 reduce-scatter.8.cloned.1.call-start
  105.4 0.7 copy-done.3
  106.1 0.2 copy-done.2
  106.2 0.1 reshape.153
  106.3 0.0 copy-done.5
  106.3 0.2 fusion.38
  106.6 0.0 copy-done.4
  106.6 0.1 iota_compare_fusion
  106.7 62.0 %reduce-scatter.6.cloned.1.call-done = f32[1024,128]{0,1:T(8,128)} async-done(((f32[8192,128]{0,1:T(8,128)}), f32[1024,128]{0,1:T(8,128)}) %reduce-scatter.6.cloned.1.call-update) | async-done | bytes 524304 | tf_op jit(solution)/shard_map/reduce_scatter | solution.py:54
  168.7 0.0 reduce-scatter.8.cloned.1.call-update
  168.7 0.0 reduce-scatter.10.cloned.1.call-start
  168.7 0.0 copy-start.1
  168.7 2.3 fusion.37
  171.0 0.1 fusion.26
  171.1 0.3 fusion.18
  171.4 0.0 copy-done.1
  171.4 0.4 convolution_convert_fusion
  171.8 0.3 fusion.27
  172.1 37.5 %reduce-scatter.8.cloned.1.call-done = f32[128,128]{0,1:T(8,128)} async-done(((f32[1024,128]{0,1:T(8,128)}), f32[128,128]{0,1:T(8,128)}) %reduce-scatter.8.cloned.1.call-update) | async-done | bytes 65552 | tf_op jit(solution)/shard_map/reduce_scatter | solution.py:54
  209.7 1.6 copy.24
  211.2 0.0 reduce-scatter.10.cloned.1.call-update
  211.2 1.8 fusion.14
  213.1 0.6 convert_element_type.35
  213.7 29.3 %reduce-scatter.10.cloned.1.call-done = f32[64,128]{1,0:T(8,128)} async-done(((f32[128,128]{1,0:T(8,128)}), f32[64,128]{1,0:T(8,128)}) %reduce-scatter.10.cloned.1.call-update) | async-done | bytes 32784
  243.0 0.8 copy.25
  243.9 0.7 copy.19
  (7 shorter events, 0.1 us)
Async XLA Ops:
  7.2 93.2 %copy-start = (bf16[128,8192]{1,0:T(8,128)(2,1)S(1)}, bf16[128,8192]{1,0:T(8,128)(2,1)}, u32[]{:S(2)}) copy-start(bf16[128,8192]{1,0:T(8,128)(2,1)} %param.17) | copy-start | bytes 6291460
  7.2 90.0 %all-gather.3.cloned.1.call-start = ((), (), s32[]{:S(2)}) async-start(), calls=%async_computation.5 | async-start | bytes 2359296 | tf_op jit(solution)/shard_map/all_gather | solution.py:41
  57.3 14.4 %all-to-all-start.1 = ((bf16[8,8,1,2,128]{4,3,0,2,1:T(2,128)(2,1)}), bf16[8,8,1,2,128]{4,3,0,2,1:T(2,128)(2,1)S(1)}, u32[]{:S(2)}, u32[]{:S(2)}) async-start(bf16[8,8,1,2,128]{4,3,0,2,1:T(2,128)(2,1)} %copy.17), calls=%async_computation.1 | async-start | bytes 65536 | tf_op jit(solution)/shard_map/all_to_all | solution.py:29
  64.8 103.8 %reduce-scatter.6.cloned.1.call-start = ((), (), s32[]{:S(2)}) async-start(), calls=%async_computation.6 | async-start | bytes 4718592 | tf_op jit(solution)/shard_map/reduce_scatter | solution.py:54
  105.3 0.7 copy-start.3
  105.3 0.9 copy-start.2
  105.3 1.0 copy-start.5
  105.3 1.3 copy-start.4
  105.3 104.3 %reduce-scatter.8.cloned.1.call-start = ((), (), s32[]{:S(2)}) async-start(), calls=%async_computation.7 | async-start | bytes 589824 | tf_op jit(solution)/shard_map/reduce_scatter | solution.py:54
  168.7 74.3 %reduce-scatter.10.cloned.1.call-start = ((), (), s32[]{:S(2)}) async-start(), calls=%async_computation.8 | async-start | bytes 98304
  168.7 2.7 %copy-start.1 = (bf16[8,8,2,64,128]{4,3,2,1,0:T(8,128)(2,1)S(1)}, bf16[8,8,2,64,128]{4,3,2,1,0:T(8,128)(2,1)}, u32[]{:S(2)}) copy-start(bf16[8,8,2,64,128]{4,3,2,1,0:T(8,128)(2,1)} %copy.16) | copy-start | bytes 6291460
Sparse Core Ops, SparseCore 0:
  44.4 52.6 all-gather.2
  105.5 63.1 reduce-scatter.5
  172.1 37.5 reduce-scatter.7
  212.8 30.1 reduce-scatter.9
where the time goes:
time: 252 us; the launch traced here: 251 us
  waiting for transfers between devices  160 us (63%)
  blocking collectives  49.4 us (20%)
  between operations  13.9 us (6%)
  matrix products  9.94 us (4%)
  local copies, waits for them, and re-layouts  9.47 us (4%)
  starting transfers between devices  7.64 us (3%)
    reduce_scatter x2, waiting for transfers between devices, own_rows(): running = lax.psum_scatter(running, axis, scatter_dimension=0, tiled=True)  99.5 us
    all_gather x2, blocking collectives, gather_in_order(): blocks = lax.all_gather(blocks, axes[k], axis=0, tiled=True)  37 us
    unnamed x5, waiting for transfers between devices  29.4 us
    all_gather x1, waiting for transfers between devices, gather_in_order(): blocks = lax.all_gather(blocks, axes[k], axis=0, tiled=True)  24.5 us
    all_to_all x1, blocking collectives, turned_blocks(): out = lax.all_to_all(out, axes[k], k, k, tiled=True)  12.4 us
    all_to_all x1, starting transfers between devices, turned_blocks(): out = lax.all_to_all(out, axes[k], k, k, tiled=True)  7.48 us
    all_to_all x1, waiting for transfers between devices, turned_blocks(): out = lax.all_to_all(out, axes[k], k, k, tiled=True)  6.17 us
  transfers between devices with their start and end apart: 5, of which 5 were waited for; matrix products, arithmetic and copies ran while one was open for 3% of the time, Pallas kernels for 0%

commit v1 on v0

--- a/solution.py
+++ b/solution.py
@@ -9,50 +9,6 @@
 NEW = 4
 DP = ("dp_0", "dp_1")
 DP_SECTION = ("dp_0", "dp_1", "section")
-
-
-def split_up(shard, dim, peers):
-    before, after = (shard.shape[:dim], shard.shape[dim + 1 :])
-    return jnp.moveaxis(shard.reshape(*before, peers, -1, *after), dim, 0)
-
-
-def laid_out(blocks, dim):
-    blocks = jnp.moveaxis(blocks, 0, dim)
-    lengths = blocks.shape
-    return blocks.reshape(*lengths[:dim], lengths[dim] * lengths[dim + 1], *lengths[dim + 2 :])
-
-
-def turned_blocks(blocks, axes, sequence):
-    inside = blocks.shape[1:]
-    out = blocks.reshape(*(lax.axis_size(a) for a in axes), *inside)
-    for k in sequence:
-        out = lax.all_to_all(out, axes[k], k, k, tiled=True)
-    return out.reshape(-1, *inside)
-
-
-def stepwise_exchange(shard, axes, sequence, split_dim, concat_dim):
-    blocks = split_up(shard, split_dim, lax.axis_size(axes))
-    return laid_out(turned_blocks(blocks, axes, sequence), concat_dim)
-
-
-def gather_in_order(shard, axes, sequence):
-    blocks = shard[None]
-    for k in sequence:
-        blocks = lax.all_gather(blocks, axes[k], axis=0, tiled=True)
-    current = [lax.axis_size(axes[k]) for k in reversed(sequence)]
-    blocks = blocks.reshape(*current, *shard.shape)
-    turned = sorted(range(len(sequence)), key=lambda place: sequence[len(sequence) - 1 - place])
-    return blocks.transpose(*turned, *range(len(sequence), blocks.ndim)).reshape(-1, *shard.shape)
-
-
-def whole_of(shard, axes, sequence, dim):
-    return laid_out(gather_in_order(shard, axes, sequence), dim)
-
-
-def own_rows(running, axes):
-    for axis in axes:
-        running = lax.psum_scatter(running, axis, scatter_dimension=0, tiled=True)
-    return running
 
 
 def per_device(
@@ -68,31 +24,41 @@
     value_target,
 ):
     replicas = lax.axis_size(DP)
-    row_count = sampled_rows.shape[0]
+    groups = lax.axis_size(DP_SECTION)
+    sections = groups // replicas
+    section = lax.axis_index("section")
+    row_count, width = sampled_rows.shape
     per_peer = row_count // replicas
+    w_rows, width_local = w_value.shape
     order = mb_map[0]
-    pieces = value_target.reshape(replicas, per_peer, value_target.shape[1])
-    returned = stepwise_exchange(pieces, DP, (0, 1), 0, 0).reshape(row_count, value_target.shape[1])
-    train_target = jnp.zeros_like(returned).at[order].set(returned)
+    pieces = value_target.reshape(replicas, 1, per_peer, width_local)
+    same = (jnp.arange(sections) == section)[None, :, None, None]
+    pieces = jnp.where(same, pieces, jnp.zeros_like(pieces)).reshape(groups, per_peer, width_local)
+    outgoing = jnp.concatenate(
+        [jnp.broadcast_to(w_value[None], (groups, w_rows, width_local)), pieces], axis=1
+    )
+    arrived = lax.all_to_all(outgoing, DP_SECTION, 0, 0, tiled=True)
+    piece = arrived[:, :w_rows].reshape(width, width_local)
+    returned = arrived[:, w_rows:].reshape(replicas, sections, per_peer, width_local)
+    returned = jnp.sum(jnp.where(same, returned, jnp.zeros_like(returned)), axis=1)
+    returned = returned.reshape(row_count, width_local)
+    place = (jnp.arange(row_count)[:, None] == order[None, :]).astype(jnp.bfloat16)
+    train_target = jnp.dot(place, returned, preferred_element_type=jnp.float32)
     prompts = hidden_new.shape[0]
-    width_local = w_value.shape[1]
     new_rows = hidden_new.reshape(prompts * NEW, hidden_new.shape[2])
-    piece = whole_of(w_value, DP_SECTION, (2, 0, 1), 0)
     v_new_full = jnp.dot(new_rows, piece, preferred_element_type=jnp.float32)
     v_train = jnp.dot(sampled_rows, piece, preferred_element_type=jnp.float32)
-    residual_value = (v_train - train_target.astype(jnp.float32)).astype(jnp.bfloat16)
-    grad_value = (
-        own_rows(
-            lax.dot_general(
-                sampled_rows,
-                residual_value,
-                (((0,), (0,)), ((), ())),
-                preferred_element_type=jnp.float32,
-            ),
-            DP_SECTION,
-        )
-        / row_count
+    residual_value = (v_train - train_target).astype(jnp.bfloat16)
+    product = lax.dot_general(
+        sampled_rows,
+        residual_value,
+        (((0,), (0,)), ((), ())),
+        preferred_element_type=jnp.float32,
+    ).astype(jnp.bfloat16)
+    terms = lax.all_to_all(
+        product.reshape(groups, w_rows, width_local), DP_SECTION, 0, 0, tiled=True
     )
+    grad_value = jnp.sum(terms.astype(jnp.float32), axis=0) / row_count
     heads_local = width_local // HD
     cache_size = key_cache.shape[1]
     scale = 1.0 / jnp.sqrt(jnp.float32(HD))

time: 252 us -> 166 us (0.66)
  the two profiles are of different devices: /device:TPU:1 before, /device:TPU:2 now
where the time goes in v1:
time: 166 us
  blocking collectives  88.1 us (53%)
  waiting for transfers between devices  48.1 us (29%)
  starting transfers between devices  8.71 us (5%)
  matrix products  8.04 us (5%)
  local copies, waits for them, and re-layouts  7.13 us (4%)
  other arithmetic  4.72 us (3%)
    all_to_all x1, blocking collectives, per_device(): arrived = lax.all_to_all(outgoing, DP_SECTION, 0, 0, tiled=True)  88.1 us
    all_to_all x1, waiting for transfers between devices, per_device(): lax.all_to_all(product.reshape(groups, w_rows, width_local), DP_SECTION,...  48.1 us
    all_to_all x1, starting transfers between devices, per_device(): lax.all_to_all(product.reshape(groups, w_rows, width_local), DP_SECTION,...  8.71 us
    convert_element_type x1, local copies, waits for them, and re-layouts, per_device(): product = lax.dot_general(sampled_rows, residual_value, (((0,), (0,)), ((...  4.08 us
  transfers between devices with their start and end apart: 1, of which 1 were waited for; matrix products, arithmetic and copies ran while one was open for 4% of the time, Pallas kernels for 0%

profile of v1, /device:TPU:2, one launch (start us, length us, event | category | flops | bytes accessed | tf_op | source)
XLA Modules:
  0.0 165.7 jit_solution(16661996735535987479)
XLA Ops:
  0.6 0.0 copy-start
  0.7 0.1 broadcast_in_dim.107
  0.8 1.1 broadcast_select_fusion.1
  1.9 1.2 broadcast_in_dim.105
  3.1 0.3 pad_maximum_fusion
  3.5 88.1 %all_to_all.10 = bf16[128,66,128]{2,1,0:T(8,128)(2,1)S(1)} all-to-all(bf16[128,66,128]{2,1,0:T(8,128)(2,1)S(1)} %pad_maximum_fusion), channel_id=1, replica_groups=mesh['dp_0'=8,'dp_1'=8,'tensor'=8,'section'=2] {'dp_0','dp_1','section'}, dimensions={0} | all-to-all | bytes 4325376 | tf_op jit(solution)/shard_map/all_to_all | solution.py:40
  91.7 0.2 fusion.25
  92.0 0.3 slice.8
  92.3 0.0 copy-start.1
  92.3 0.0 copy-done
  92.3 0.0 copy-start.5
  92.3 0.8 convolution_bitcast_fusion
  93.1 0.6 copy-done.1
  93.6 0.0 copy-done.5
  93.6 2.2 %fusion = bf16[8192,128]{0,1:T(8,128)(2,1)} fusion(bf16[128,8192]{1,0:T(8,128)(2,1)S(1)} %copy-done, f32[128,128]{0,1:T(8,128)S(1)} %convolution_bitcast_fusion, bf16[128,128]{1,0:T(8,128)(2,1)S(1)} %bitcast.72, s32[128]{0:T(128)S(1)} %bitcast.74), kind=kOutput, calls=%fused_computation.1 | convolution fusion | flops 273727488 | bytes 4293120 | tf_op jit(solution)/shard_map/dot_general | solution.py:52
  95.8 4.1 %copy.24 = bf16[8192,128]{1,0:T(8,128)(2,1)} copy(bf16[8192,128]{0,1:T(8,128)(2,1)} %fusion) | data formatting | bytes 4194304 | tf_op jit(solution)/shard_map/convert_element_type | solution.py:57
  99.9 0.0 copy-start.4
  99.9 0.0 copy-start.3
  99.9 0.0 copy-start.7
  99.9 0.0 copy-start.6
  99.9 8.7 %all-to-all-start.1 = ((bf16[128,64,128]{2,1,0:T(8,128)(2,1)}), bf16[128,64,128]{2,1,0:T(8,128)(2,1)}, u32[]{:S(2)}, u32[]{:S(2)}) async-start(bf16[128,64,128]{2,1,0:T(8,128)(2,1)} %bitcast.70), calls=%async_computation.1 | async-start | bytes 4194304 | tf_op jit(solution)/shard_map/all_to_all | solution.py:58
  108.6 0.0 copy-done.4
  108.7 0.0 copy-done.3
  108.7 0.1 reshape.146
  108.7 0.0 copy-start.2
  108.8 0.0 copy-done.7
  108.8 0.2 fusion.39
  109.0 0.0 copy-done.6
  109.0 0.1 iota_compare_fusion.3
  109.1 2.3 %fusion.38 = (f32[3,4,8]{2,1,0:T(4,128)S(1)}, f32[3,4,8,2048]{3,2,1,0:T(8,128)S(1)}) fusion(bf16[3,4,8,128]{3,2,1,0:T(8,128)(2,1)S(1)} %reshape.144, bf16[3,2048,128]{2,1,0:T(8,128)(2,1)} %param.14, pred[3,2048]{1,0:T(4,128)(4,1)S(1)} %iota_compare_fusion.3), kind=kOutput, calls=%fused_computation.48 | convolution fusion | flops 50921376 | bytes 2390400 | tf_op jit(solution)/shard_map/ptgqd,pjgd->pgtqj/dot_general | solution.py:71
  111.4 0.1 fusion.28
  111.5 0.3 fusion.20
  111.8 0.0 copy-done.2
  111.8 0.4 fusion.19
  112.3 0.3 fusion.29
  112.5 1.9 %fusion.15 = bf16[3,4,1,8,128]{4,3,1,0,2:T(8,128)(2,1)S(1)} fusion(f32[3,128,4,8]{1,3,2,0:T(8,128)S(1)} %fusion.29, bf16[3,2048,128]{2,1,0:T(8,128)(2,1)} %param.15, f32[3,4,8,2048]{3,2,1,0:T(8,128)S(1)} %get-tuple-element.3, f32[3,4,8]{2,1,0:T(4,128)S(1)} %add.13, f32[3,4,8]{2,1,0:T(4,128)S(1)} %max.9, pred[3,2048]{1,0:T(4,128)(4,1)S(1)} %iota_compare_fusion.3), kind=kOutput, calls=%fused_computation.15 | convolution fusion | flops 51142656 | bytes 2439936 | tf_op jit(solution)/shard_map/pgtqj,pjgd->ptgqd/dot_general | solution.py:88
  114.4 0.6 convert_element_type.48
  115.0 48.1 %all-to-all-done.1 = bf16[128,64,128]{2,1,0:T(8,128)(2,1)} async-done(((bf16[128,64,128]{2,1,0:T(8,128)(2,1)}), bf16[128,64,128]{2,1,0:T(8,128)(2,1)}, u32[]{:S(2)}, u32[]{:S(2)}) %all-to-all-start.1) | async-done | bytes 2097184 | tf_op jit(solution)/shard_map/all_to_all | solution.py:58
  163.1 2.0 %convert_reduce_fusion = f32[64,128]{1,0:T(8,128)S(1)} fusion(bf16[128,64,128]{2,1,0:T(8,128)(2,1)} %all-to-all-done.1), kind=kLoop, calls=%fused_computation.2 | loop fusion | flops 2088960 | bytes 2129920 | tf_op jit(solution)/shard_map/reduce_sum | solution.py:61
  165.1 0.6 broadcast_multiply_fusion
  (10 shorter events, 0.2 us)
Async XLA Ops:
  0.6 91.6 %copy-start = (bf16[128,8192]{1,0:T(8,128)(2,1)S(1)}, bf16[128,8192]{1,0:T(8,128)(2,1)}, u32[]{:S(2)}) copy-start(bf16[128,8192]{1,0:T(8,128)(2,1)} %param.17) | copy-start | bytes 6291460
  92.3 1.4 copy-start.1
  92.3 1.3 copy-start.5
  99.9 8.7 %copy-start.4 = (bf16[3,4,1024]{2,1,0:T(4,128)(2,1)S(1)}, bf16[3,4,1024]{2,1,0:T(4,128)(2,1)}, u32[]{:S(2)}) copy-start(bf16[3,4,1024]{2,1,0:T(4,128)(2,1)} %param.12) | copy-start | bytes 73732
  99.9 8.8 %copy-start.3 = (bf16[3,4,8192]{2,1,0:T(4,128)(2,1)S(1)}, bf16[3,4,8192]{2,1,0:T(4,128)(2,1)}, u32[]{:S(2)}) copy-start(bf16[3,4,8192]{2,1,0:T(4,128)(2,1)} %param.11) | copy-start | bytes 589828
  99.9 8.9 %copy-start.7 = (bf16[3,4,128]{2,1,0:T(4,128)(2,1)S(1)}, bf16[3,4,128]{2,1,0:T(4,128)(2,1)}, u32[]{:S(2)}) copy-start(bf16[3,4,128]{2,1,0:T(4,128)(2,1)} %param.13) | copy-start | bytes 9220
  99.9 9.1 %copy-start.6 = (s32[3]{0:T(128)S(1)}, s32[3]{0:T(128)}, u32[]{:S(2)}) copy-start(s32[3]{0:T(128)} %param.16) | copy-start | bytes 40
  99.9 63.2 %all-to-all-start.1 = ((bf16[128,64,128]{2,1,0:T(8,128)(2,1)}), bf16[128,64,128]{2,1,0:T(8,128)(2,1)}, u32[]{:S(2)}, u32[]{:S(2)}) async-start(bf16[128,64,128]{2,1,0:T(8,128)(2,1)} %bitcast.70), calls=%async_computation.1 | async-start | bytes 4194304 | tf_op jit(solution)/shard_map/all_to_all | solution.py:58
  108.7 3.1 %copy-start.2 = (bf16[128,64,128]{2,1,0:T(8,128)(2,1)S(1)}, bf16[128,64,128]{2,1,0:T(8,128)(2,1)}, u32[]{:S(2)}) copy-start(bf16[128,64,128]{2,1,0:T(8,128)(2,1)} %copy-done.1) | copy-start | bytes 6291460

commit v2 on v1

--- a/solution.py
+++ b/solution.py
@@ -1,14 +1,128 @@
 import jax
 import jax.numpy as jnp
 from jax import lax
+from jax.experimental import pallas as pl
+from jax.experimental.pallas import tpu as pltpu
 from jax.sharding import Mesh
 from jax.sharding import PartitionSpec as P
 
 HD = 128
 QPK = 8
 NEW = 4
+LANES = 128
+PAD = 16
 DP = ("dp_0", "dp_1")
 DP_SECTION = ("dp_0", "dp_1", "section")
+
+
+def picker(section, w_rows):
+    row = lax.broadcasted_iota(jnp.int32, (2 * LANES, LANES), 0)
+    col = lax.broadcasted_iota(jnp.int32, (2 * LANES, LANES), 1)
+    source = (col // w_rows) * (2 * w_rows) + col % w_rows + section * w_rows
+    return (row == source).astype(jnp.float32).astype(jnp.bfloat16)
+
+
+def halves_body(where_ref, rows_ref, new_ref, keep_ref, send_ref, *, w_rows):
+    section, core = where_ref[0], where_ref[1]
+    half = rows_ref.shape[0] // 2
+    sent_at = pl.ds(pl.multiple_of(core * half, half), half)
+    own = picker(section, w_rows)
+    other = picker(1 - section, w_rows)
+    row_count = rows_ref.shape[0]
+
+    def pick(block, which):
+        return jnp.dot(block, which, preferred_element_type=jnp.float32).astype(jnp.bfloat16)
+
+    for tile in range(rows_ref.shape[1] // (2 * LANES)):
+        wide = slice(tile * 2 * LANES, (tile + 1) * 2 * LANES)
+        thin = slice(tile * LANES, (tile + 1) * LANES)
+        keep_ref[:row_count, thin] = pick(rows_ref[:, wide], own)
+        keep_ref[row_count:, thin] = pick(new_ref[:, wide], own)
+        send_ref[:half, thin] = pick(rows_ref[sent_at, wide], other)
+        send_ref[half:, thin] = pick(new_ref[:, wide], other)
+
+
+def split_halves(where, rows, new_rows, w_rows):
+    row_count, width = rows.shape
+    steps = 4
+    block = width // steps
+    kept, sent = row_count + PAD, row_count // 2 + PAD
+    return pl.pallas_call(
+        lambda *refs: halves_body(*refs, w_rows=w_rows),
+        grid=(steps,),
+        in_specs=[
+            pl.BlockSpec(memory_space=pltpu.SMEM),
+            pl.BlockSpec((row_count, block), lambda i: (0, i)),
+            pl.BlockSpec((PAD, block), lambda i: (0, i)),
+        ],
+        out_specs=[
+            pl.BlockSpec((kept, block // 2), lambda i: (0, i)),
+            pl.BlockSpec((sent, block // 2), lambda i: (0, i)),
+        ],
+        out_shape=[
+            jax.ShapeDtypeStruct((kept, width // 2), jnp.bfloat16),
+            jax.ShapeDtypeStruct((sent, width // 2), jnp.bfloat16),
+        ],
+        cost_estimate=pl.CostEstimate(
+            flops=2 * (kept + sent) * width * LANES,
+            bytes_accessed=4 * (row_count + PAD) * width,
+            transcendentals=0,
+        ),
+        name="halves",
+    )(where, rows, new_rows)
+
+
+def product_body(kept_ref, first_ref, second_ref, own_ref, res1_ref, res2_ref, out_ref):
+    half = res1_ref.shape[0]
+    own_rows = own_ref.shape[0]
+    contract = (((0,), (0,)), ((), ()))
+
+    def term(rows, residual):
+        return lax.dot_general(rows, residual, contract, preferred_element_type=jnp.float32)
+
+    total = term(kept_ref[:own_rows, :], own_ref[...])
+    total += term(first_ref[:half, :], res1_ref[...])
+    total += term(second_ref[:half, :], res2_ref[...])
+    out_ref[...] = total.astype(out_ref.dtype)
+
+
+def weight_product(kept, first, second, res_own, res1, res2):
+    width = kept.shape[1]
+    columns = res_own.shape[1]
+    steps = 4
+    block = width // steps
+
+    def whole(x):
+        return pl.BlockSpec(x.shape, lambda i: (0, 0))
+
+    return pl.pallas_call(
+        product_body,
+        grid=(steps,),
+        in_specs=[
+            pl.BlockSpec((kept.shape[0], block), lambda i: (0, i)),
+            pl.BlockSpec((first.shape[0], block), lambda i: (0, i)),
+            pl.BlockSpec((second.shape[0], block), lambda i: (0, i)),
+            whole(res_own),
+            whole(res1),
+            whole(res2),
+        ],
+        out_specs=pl.BlockSpec((block, columns), lambda i: (i, 0)),
+        out_shape=jax.ShapeDtypeStruct((width, columns), jnp.bfloat16),
+        cost_estimate=pl.CostEstimate(
+            flops=4 * width * columns * res_own.shape[0],
+            bytes_accessed=2 * width * (kept.shape[0] + 2 * first.shape[0] + columns),
+            transcendentals=0,
+        ),
+        name="product",
+    )(kept, first, second, res_own, res1, res2)
+
+
+def swap_section(x):
+    return lax.ppermute(x, "section", [(0, 1), (1, 0)])
+
+
+def swap_core(x):
+    return lax.ppermute(x, "tensor", [(i, i ^ 1) for i in range(lax.axis_size("tensor"))])
 
 
 def per_device(
@@ -24,45 +138,62 @@
     value_target,
 ):
     replicas = lax.axis_size(DP)
-    groups = lax.axis_size(DP_SECTION)
-    sections = groups // replicas
     section = lax.axis_index("section")
-    row_count, width = sampled_rows.shape
+    core = lax.axis_index("tensor") % 2
+    row_count = sampled_rows.shape[0]
+    half = row_count // 2
     per_peer = row_count // replicas
     w_rows, width_local = w_value.shape
     order = mb_map[0]
-    pieces = value_target.reshape(replicas, 1, per_peer, width_local)
-    same = (jnp.arange(sections) == section)[None, :, None, None]
-    pieces = jnp.where(same, pieces, jnp.zeros_like(pieces)).reshape(groups, per_peer, width_local)
+    prompts = hidden_new.shape[0]
+    new_count = prompts * NEW
+    new_rows = hidden_new.reshape(new_count, hidden_new.shape[2])
+    new_rows = jnp.pad(new_rows, ((0, PAD - new_count), (0, 0)))
+
+    where = jnp.stack([section, core]).astype(jnp.int32)
+    kept, sent = split_halves(where, sampled_rows, new_rows, w_rows)
+    first = swap_section(sent)
+
+    pieces = jnp.pad(value_target.reshape(replicas, per_peer, width_local), ((0, 0), (0, 8 - per_peer), (0, 0)))
     outgoing = jnp.concatenate(
-        [jnp.broadcast_to(w_value[None], (groups, w_rows, width_local)), pieces], axis=1
-    )
-    arrived = lax.all_to_all(outgoing, DP_SECTION, 0, 0, tiled=True)
-    piece = arrived[:, :w_rows].reshape(width, width_local)
-    returned = arrived[:, w_rows:].reshape(replicas, sections, per_peer, width_local)
-    returned = jnp.sum(jnp.where(same, returned, jnp.zeros_like(returned)), axis=1)
-    returned = returned.reshape(row_count, width_local)
+        [jnp.broadcast_to(w_value[None], (replicas, w_rows, width_local)), pieces], axis=1
+    )
+    arrived = lax.all_to_all(outgoing, DP, 0, 0, tiled=True)
+    second = swap_core(first)
+    piece = arrived[:, :w_rows].reshape(replicas * w_rows, width_local)
+    returned = arrived[:, w_rows : w_rows + per_peer].reshape(row_count, width_local)
     place = (jnp.arange(row_count)[:, None] == order[None, :]).astype(jnp.bfloat16)
     train_target = jnp.dot(place, returned, preferred_element_type=jnp.float32)
-    prompts = hidden_new.shape[0]
-    new_rows = hidden_new.reshape(prompts * NEW, hidden_new.shape[2])
-    v_new_full = jnp.dot(new_rows, piece, preferred_element_type=jnp.float32)
-    v_train = jnp.dot(sampled_rows, piece, preferred_element_type=jnp.float32)
-    residual_value = (v_train - train_target).astype(jnp.bfloat16)
-    product = lax.dot_general(
-        sampled_rows,
-        residual_value,
-        (((0,), (0,)), ((), ())),
-        preferred_element_type=jnp.float32,
-    ).astype(jnp.bfloat16)
+
+    def times(rows):
+        return jnp.dot(rows, piece, preferred_element_type=jnp.float32)
+
+    v_kept, v_first, v_second = times(kept), times(first), times(second)
+    mine = v_kept[:row_count] - train_target
+    upper = core == 1
+    theirs = jnp.concatenate(
+        [
+            jnp.where(upper, v_second[:half], v_first[:half]),
+            jnp.where(upper, v_first[:half], v_second[:half]),
+        ],
+        axis=0,
+    )
+    partial = jnp.concatenate([mine, theirs, v_first[half:]], axis=0)
+    other = swap_section(partial)
+    res_own = (mine + other[row_count : 2 * row_count]).astype(jnp.bfloat16)
+    res_their = (theirs + other[:row_count]).astype(jnp.bfloat16)
+    v_new_rows = (v_kept[row_count:] + other[2 * row_count :])[:new_count]
+    res1 = jnp.where(upper, res_their[half:], res_their[:half])
+    res2 = jnp.where(upper, res_their[:half], res_their[half:])
+    product = weight_product(kept, first, second, res_own, res1, res2)
     terms = lax.all_to_all(
-        product.reshape(groups, w_rows, width_local), DP_SECTION, 0, 0, tiled=True
+        product.reshape(replicas, w_rows, width_local), DP, 0, 0, tiled=True
     )
     grad_value = jnp.sum(terms.astype(jnp.float32), axis=0) / row_count
     heads_local = width_local // HD
     cache_size = key_cache.shape[1]
     scale = 1.0 / jnp.sqrt(jnp.float32(HD))
-    v_new = v_new_full.astype(jnp.bfloat16).reshape(prompts, NEW, heads_local, HD)
+    v_new = v_new_rows.astype(jnp.bfloat16).reshape(prompts, NEW, heads_local, HD)
     query_h = query.reshape(prompts, NEW, heads_local, QPK, HD)
     kc_heads = key_cache.reshape(prompts, cache_size, heads_local, HD)
     vc_heads = value_cache.reshape(prompts, cache_size, heads_local, HD)

time: 166 us -> 136 us (0.82)
  the two profiles are of different devices: /device:TPU:2 before, /device:TPU:4 now
where the time goes in v2:
time: 136 us; the launch traced here: 135 us
  starting transfers between devices  64.6 us (47%)
  waiting for transfers between devices  45.1 us (33%)
  Pallas kernels  9.17 us (7%)
  matrix products  5.37 us (4%)
  other arithmetic  5.07 us (4%)
  local copies, waits for them, and re-layouts  4.79 us (4%)
    ppermute x2, starting transfers between devices, swap_section(): return lax.ppermute(x, 'section', [(0, 1), (1, 0)])  31.6 us
    all_to_all x1, waiting for transfers between devices, per_device(): lax.all_to_all(product.reshape(replicas, w_rows, width_local), DP, 0, 0,...  26.2 us
    ppermute x2, waiting for transfers between devices, swap_section(): return lax.ppermute(x, 'section', [(0, 1), (1, 0)])  18.9 us
    all_to_all x1, starting transfers between devices, per_device(): arrived = lax.all_to_all(outgoing, DP, 0, 0, tiled=True)  18.2 us
    all_to_all x1, starting transfers between devices, per_device(): lax.all_to_all(product.reshape(replicas, w_rows, width_local), DP, 0, 0,...  12.8 us
    pallas_call x1, Pallas kernels, split_halves(): pl.pallas_call(lambda *refs: halves_body(*refs, w_rows=w_rows), grid=(ste...  4.75 us
    pallas_call x1, Pallas kernels, weight_product(): pl.pallas_call(product_body, grid=(steps,), in_specs=[pl.BlockSpec((kept....  4.43 us
  transfers between devices with their start and end apart: 5, of which 3 were waited for; matrix products, arithmetic and copies ran while one was open for 7% of the time, Pallas kernels for 4%

profile of v2, /device:TPU:4, one launch (start us, length us, event | category | flops | bytes accessed | tf_op | source)
XLA Modules:
  0.0 135.0 jit_solution(626305557173440522)
XLA Ops:
  0.6 0.0 copy-start
  0.6 1.1 broadcast_in_dim.60
  1.7 1.9 %fusion.5 = bf16[64,72,128]{2,1,0:T(8,128)(2,1)} fusion(bf16[64,2,128]{2,1,0:T(2,128)(2,1)} %bitcast.66, bf16[64,64,128]{2,1,0:T(8,128)(2,1)S(1)} %broadcast_in_dim.60), kind=kLoop, calls=%fused_computation.8 | loop fusion | flops 3538944 | bytes 2260992 | tf_op jit(solution)/shard_map/concatenate | solution.py:158
  3.6 0.0 copy-start.3
  3.6 18.2 %all-to-all-start = ((bf16[64,72,128]{2,1,0:T(8,128)(2,1)}), bf16[64,72,128]{2,1,0:T(8,128)(2,1)}, u32[]{:S(2)}, u32[]{:S(2)}) async-start(bf16[64,72,128]{2,1,0:T(8,128)(2,1)} %fusion.5), calls=%async_computation | async-start | bytes 2359296 | tf_op jit(solution)/shard_map/all_to_all | solution.py:161
  21.9 0.0 copy-done.3
  21.9 0.1 reshape.135
  21.9 0.7 pad.8.refs_2_
  22.7 0.6 pad_add_fusion.refs_0_
  23.3 4.7 %halves.1 = (bf16[144,4096]{1,0:T(8,128)(2,1)}, bf16[80,4096]{1,0:T(8,128)(2,1)}) custom-call(s32[2]{0:T(128)} %pad_add_fusion.refs_0_, bf16[128,8192]{1,0:T(8,128)(2,1)} %refs_1_.1, bf16[16,8192]{1,0:T(8,128)(2,1)} %pad.8.refs_2_), custom_call_target="tpu_custom_call" | custom-call | flops 469762048 | bytes 4718592 | tf_op jit(solution)/shard_map/halves/pallas_call | solution.py:50
  28.0 10.2 %collective-permute-start = (bf16[80,4096]{1,0:T(8,128)(2,1)}, bf16[80,4096]{1,0:T(8,128)(2,1)S(1)}, u32[]{:S(2)}, u32[]{:S(2)}) collective-permute-start(bf16[80,4096]{1,0:T(8,128)(2,1)} %get-tuple-element.5), channel_id=1, source_target_pairs={{0,1},{1,0},{2,3},{3,2},{4,5},{5,4},{6,7},{7,6},{8,9},{9,8},{10,11... | collective-permute-start | bytes 1966088 | tf_op jit(solution)/shard_map/ppermute | solution.py:121
  38.2 0.0 copy-start.1
  38.2 14.5 %collective-permute-done.first_ref = bf16[80,4096]{1,0:T(8,128)(2,1)S(1)} collective-permute-done((bf16[80,4096]{1,0:T(8,128)(2,1)}, bf16[80,4096]{1,0:T(8,128)(2,1)S(1)}, u32[]{:S(2)}, u32[]{:S(2)}) %collective-permute-start) | collective-permute-done | bytes 655392 | tf_op jit(solution)/shard_map/ppermute | solution.py:121
  52.7 0.0 copy-start.2
  52.7 1.9 %collective-permute-start.1 = (bf16[80,4096]{1,0:T(8,128)(2,1)S(1)}, bf16[80,4096]{1,0:T(8,128)(2,1)}, u32[]{:S(2)}, u32[]{:S(2)}) collective-permute-start(bf16[80,4096]{1,0:T(8,128)(2,1)S(1)} %collective-permute-done.first_ref), channel_id=1, source_target_pairs={{0,2},{2,0},{4,6},{6,4},{8,10},{10,8},{12,14},{14,12},{1,3},{3,1},... | collective-permute-start | bytes 1966088 | tf_op jit(solution)/shard_map/ppermute | solution.py:125
  54.6 0.0 all-to-all-done
  54.6 1.3 slice.58
  55.9 0.4 fusion.43
  56.3 0.0 copy-done.2
  56.3 0.0 copy-start.6
  56.3 0.9 slice.61
  57.3 0.0 copy-done.1
  57.3 0.5 fusion.42
  57.8 0.0 copy-start.5
  57.8 0.0 copy-done.6
  57.8 0.1 convolution_subtract_fusion
  57.9 0.0 collective-permute-done.1.second_ref
  57.9 1.4 %slice_select_fusion.1 = (f32[64,128]{1,0:T(8,128)S(1)}, f32[64,128]{1,0:T(8,128)S(1)}) fusion(f32[80,128]{1,0:T(8,128)S(1)} %fusion.43, pred[]{:T(512)S(6)} %eq.24, bf16[4096,128]{1,0:T(8,128)(2,1)S(1)} %bitcast.63, bf16[80,4096]{1,0:T(8,128)(2,1)} %collective-permute-done.1.second_ref), kind=kOutput, calls=%fused_computation.34 | convolution fusion | flops 67125248 | bytes 1671169 | tf_op jit(solution)/shard_map/dot_general | solution.py:169
  59.3 21.4 %collective-permute-start.2 = (f32[272,128]{1,0:T(8,128)S(1)}, f32[272,128]{1,0:T(8,128)S(1)}, u32[]{:S(2)}, u32[]{:S(2)}) collective-permute-start(f32[272,128]{1,0:T(8,128)S(1)} %pad_maximum_fusion), channel_id=1, source_target_pairs={{0,1},{1,0},{2,3},{3,2},{4,5},{5,4},{6,7},{7,6},{8,9},{9,8},{10,11... | collective-permute-start | bytes 417800 | tf_op jit(solution)/shard_map/ppermute | solution.py:121
  80.8 0.0 copy-done.5
  80.8 4.4 %collective-permute-done.2 = f32[272,128]{1,0:T(8,128)S(1)} collective-permute-done((f32[272,128]{1,0:T(8,128)S(1)}, f32[272,128]{1,0:T(8,128)S(1)}, u32[]{:S(2)}, u32[]{:S(2)}) %collective-permute-start.2) | collective-permute-done | bytes 139296 | tf_op jit(solution)/shard_map/ppermute | solution.py:121
  85.2 0.0 copy-start.4
  85.2 0.7 fusion.26
  85.9 0.6 broadcast_select_fusion
  86.5 4.4 %product.1 = bf16[4096,128]{1,0:T(8,128)(2,1)} custom-call(bf16[144,4096]{1,0:T(8,128)(2,1)} %get-tuple-element.4.kept_ref, bf16[80,4096]{1,0:T(8,128)(2,1)} %copy-done.2, bf16[80,4096]{1,0:T(8,128)(2,1)} %collective-permute-done.1.second_ref, bf16[128,128]{1,0:T(8,128)(2,1)} %get-tuple-element.7.own_ref, bf16[64,128]{1,0:T(8,128)(2,1)} %get-tuple-element.11.res1_ref, ...), custom_call_target="tpu_custom_call" | custom-call | flops 268435456 | bytes 3538944 | tf_op jit(solution)/shard_map/product/pallas_call | solution.py:98
  90.9 0.0 copy-done.4
  90.9 0.0 copy-start.8
  90.9 0.0 copy-start.7
  90.9 12.8 %all-to-all-start.1 = ((bf16[64,64,128]{2,1,0:T(8,128)(2,1)}), bf16[64,64,128]{2,1,0:T(8,128)(2,1)S(1)}, u32[]{:S(2)}, u32[]{:S(2)}) async-start(bf16[64,64,128]{2,1,0:T(8,128)(2,1)} %bitcast.64), calls=%async_computation.1 | async-start | bytes 2097152 | tf_op jit(solution)/shard_map/all_to_all | solution.py:189
  103.8 0.0 copy-done.8
  103.8 0.2 fusion.41
  104.0 0.0 copy-done.7
  104.0 0.1 iota_compare_fusion.3
  104.1 0.0 copy-done
  104.1 0.0 slice-start
  104.1 0.7 fusion.40
  104.9 0.1 fusion.29
  105.0 0.3 fusion.19
  105.3 0.0 slice-done
  105.3 0.3 fusion.30
  105.6 1.8 %fusion.15 = bf16[3,4,1,8,128]{4,3,1,0,2:T(8,128)(2,1)S(1)} fusion(f32[3,128,4,8]{1,3,2,0:T(8,128)S(1)} %fusion.30, bf16[3,2048,128]{2,1,0:T(8,128)(2,1)} %param.15, f32[3,4,8,2048]{3,2,1,0:T(8,128)S(1)} %get-tuple-element.13, f32[3,4,8]{2,1,0:T(4,128)S(1)} %add.30, f32[3,4,8]{2,1,0:T(4,128)S(1)} %max.9, pred[3,2048]{1,0:T(4,128)(4,1)S(1)} %iota_compare_fusion.3), kind=kOutput, calls=%fused_computation.13 | convolution fusion | flops 51142656 | bytes 2439936 | tf_op jit(solution)/shard_map/pgtqj,pjgd->ptgqd/dot_general | solution.py:219
  107.4 0.6 convert_element_type.40
  108.0 26.2 %all-to-all-done.1 = bf16[64,64,128]{2,1,0:T(8,128)(2,1)S(1)} async-done(((bf16[64,64,128]{2,1,0:T(8,128)(2,1)}), bf16[64,64,128]{2,1,0:T(8,128)(2,1)S(1)}, u32[]{:S(2)}, u32[]{:S(2)}) %all-to-all-start.1) | async-done | bytes 1048608 | tf_op jit(solution)/shard_map/all_to_all | solution.py:189
  134.2 0.2 convert_reduce_fusion
  134.4 0.6 broadcast_multiply_fusion
  (9 shorter events, 0.1 us)
Async XLA Ops:
  0.6 103.5 %copy-start = (bf16[3,2048,128]{2,1,0:T(8,128)(2,1)S(1)}, bf16[3,2048,128]{2,1,0:T(8,128)(2,1)}, u32[]{:S(2)}) copy-start(bf16[3,2048,128]{2,1,0:T(8,128)(2,1)} %param.14) | copy-start | bytes 4718596
  3.6 18.2 %copy-start.3 = (bf16[3,4,8192]{2,1,0:T(4,128)(2,1)S(1)}, bf16[3,4,8192]{2,1,0:T(4,128)(2,1)}, u32[]{:S(2)}) copy-start(bf16[3,4,8192]{2,1,0:T(4,128)(2,1)} %param.11) | copy-start | bytes 589828
  3.6 51.0 %all-to-all-start = ((bf16[64,72,128]{2,1,0:T(8,128)(2,1)}), bf16[64,72,128]{2,1,0:T(8,128)(2,1)}, u32[]{:S(2)}, u32[]{:S(2)}) async-start(bf16[64,72,128]{2,1,0:T(8,128)(2,1)} %fusion.5), calls=%async_computation | async-start | bytes 2359296 | tf_op jit(solution)/shard_map/all_to_all | solution.py:161
  28.0 24.7 %collective-permute-start = (bf16[80,4096]{1,0:T(8,128)(2,1)}, bf16[80,4096]{1,0:T(8,128)(2,1)S(1)}, u32[]{:S(2)}, u32[]{:S(2)}) collective-permute-start(bf16[80,4096]{1,0:T(8,128)(2,1)} %get-tuple-element.5), channel_id=1, source_target_pairs={{0,1},{1,0},{2,3},{3,2},{4,5},{5,4},{6,7},{7,6},{8,9},{9,8},{10,11... | collective-permute-start | bytes 1966088 | tf_op jit(solution)/shard_map/ppermute | solution.py:121
  38.2 19.1 %copy-start.1 = (bf16[144,4096]{1,0:T(8,128)(2,1)S(1)}, bf16[144,4096]{1,0:T(8,128)(2,1)}, u32[]{:S(2)}) copy-start(bf16[144,4096]{1,0:T(8,128)(2,1)} %get-tuple-element.4.kept_ref) | copy-start | bytes 3538948
  52.7 3.6 %copy-start.2 = (bf16[80,4096]{1,0:T(8,128)(2,1)}, bf16[80,4096]{1,0:T(8,128)(2,1)S(1)}, u32[]{:S(2)}) copy-start(bf16[80,4096]{1,0:T(8,128)(2,1)S(1)} %collective-permute-done.first_ref) | copy-start | bytes 1966084
  52.7 5.2 %collective-permute-start.1 = (bf16[80,4096]{1,0:T(8,128)(2,1)S(1)}, bf16[80,4096]{1,0:T(8,128)(2,1)}, u32[]{:S(2)}, u32[]{:S(2)}) collective-permute-start(bf16[80,4096]{1,0:T(8,128)(2,1)S(1)} %collective-permute-done.first_ref), channel_id=1, source_target_pairs={{0,2},{2,0},{4,6},{6,4},{8,10},{10,8},{12,14},{14,12},{1,3},{3,1},... | collective-permute-start | bytes 1966088 | tf_op jit(solution)/shard_map/ppermute | solution.py:125
  56.3 1.5 %copy-start.6 = (s32[1,128]{1,0:T(1,128)S(1)}, s32[1,128]{1,0:T(1,128)}, u32[]{:S(2)}) copy-start(s32[1,128]{1,0:T(1,128)} %param.18) | copy-start | bytes 1540
  57.8 23.0 %copy-start.5 = (bf16[3,4,1024]{2,1,0:T(4,128)(2,1)S(1)}, bf16[3,4,1024]{2,1,0:T(4,128)(2,1)}, u32[]{:S(2)}) copy-start(bf16[3,4,1024]{2,1,0:T(4,128)(2,1)} %param.12) | copy-start | bytes 73732
  59.3 25.9 %collective-permute-start.2 = (f32[272,128]{1,0:T(8,128)S(1)}, f32[272,128]{1,0:T(8,128)S(1)}, u32[]{:S(2)}, u32[]{:S(2)}) collective-permute-start(f32[272,128]{1,0:T(8,128)S(1)} %pad_maximum_fusion), channel_id=1, source_target_pairs={{0,1},{1,0},{2,3},{3,2},{4,5},{5,4},{6,7},{7,6},{8,9},{9,8},{10,11... | collective-permute-start | bytes 417800 | tf_op jit(solution)/shard_map/ppermute | solution.py:121
  85.2 5.7 %copy-start.4 = (f32[272,128]{1,0:T(8,128)}, f32[272,128]{1,0:T(8,128)S(1)}, u32[]{:S(2)}) copy-start(f32[272,128]{1,0:T(8,128)S(1)} %collective-permute-done.2) | copy-start | bytes 417796
  90.9 12.9 %copy-start.8 = (bf16[3,4,128]{2,1,0:T(4,128)(2,1)S(1)}, bf16[3,4,128]{2,1,0:T(4,128)(2,1)}, u32[]{:S(2)}) copy-start(bf16[3,4,128]{2,1,0:T(4,128)(2,1)} %param.13) | copy-start | bytes 9220
  90.9 13.1 %copy-start.7 = (s32[3]{0:T(128)S(1)}, s32[3]{0:T(128)}, u32[]{:S(2)}) copy-start(s32[3]{0:T(128)} %param.16) | copy-start | bytes 40
  90.9 43.3 %all-to-all-start.1 = ((bf16[64,64,128]{2,1,0:T(8,128)(2,1)}), bf16[64,64,128]{2,1,0:T(8,128)(2,1)S(1)}, u32[]{:S(2)}, u32[]{:S(2)}) async-start(bf16[64,64,128]{2,1,0:T(8,128)(2,1)} %bitcast.64), calls=%async_computation.1 | async-start | bytes 2097152 | tf_op jit(solution)/shard_map/all_to_all | solution.py:189
  104.1 1.1 slice-start

commit v3 on v2

v3 whole, which is shorter than its diff:
```python
import jax
import jax.numpy as jnp
from jax import lax
from jax.experimental import pallas as pl
from jax.experimental.pallas import tpu as pltpu
from jax.sharding import Mesh
from jax.sharding import PartitionSpec as P

HD = 128
QPK = 8
NEW = 4
LANES = 128
PAD = 16
SLOT = 8
DP = ("dp_0", "dp_1")
DP_SECTION = ("dp_0", "dp_1", "section")
F32, BF16 = jnp.float32, jnp.bfloat16


def one_hot(cond):
    return cond.astype(F32).astype(BF16)


def picker(section, w_rows):
    row = lax.broadcasted_iota(jnp.int32, (2 * LANES, LANES), 0)
    col = lax.broadcasted_iota(jnp.int32, (2 * LANES, LANES), 1)
    source = (col // w_rows) * (2 * w_rows) + col % w_rows + section * w_rows
    return one_hot(row == source)


def halves_body(where_ref, rows_ref, new_ref, w_ref, target_ref, keep_ref, send_ref, out_ref):
    section, core = where_ref[0], where_ref[1]
    row_count = rows_ref.shape[0]
    half = row_count // 2
    w_rows = w_ref.shape[0]
    sent_at = pl.ds(pl.multiple_of(core * half, half), half)
    own = picker(section, w_rows)
    other = picker(1 - section, w_rows)

    def pick(block, which):
        return jnp.dot(block, which, preferred_element_type=F32).astype(BF16)

    for tile in range(rows_ref.shape[1] // (2 * LANES)):
        wide = slice(tile * 2 * LANES, (tile + 1) * 2 * LANES)
        thin = slice(tile * LANES, (tile + 1) * LANES)
        keep_ref[:row_count, thin] = pick(rows_ref[:, wide], own)
        keep_ref[row_count:, thin] = pick(new_ref[:, wide], own)
        send_ref[:half, thin] = pick(rows_ref[sent_at, wide], other)
        send_ref[half:, thin] = pick(new_ref[:, wide], other)
    peers = out_ref.shape[0]
    targets = target_ref.shape[0]
    per_peer = targets // peers
    row = lax.broadcasted_iota(jnp.int32, (peers * SLOT, targets), 0)
    col = lax.broadcasted_iota(jnp.int32, (peers * SLOT, targets), 1)
    spread = one_hot((row % SLOT < per_peer) & (col == (row // SLOT) * per_peer + row % SLOT))
    slots = jnp.dot(spread, target_ref[...], preferred_element_type=F32)
    slots = slots.reshape(peers, SLOT, -1).astype(BF16)
    for peer in range(peers):
        out_ref[peer, :w_rows, :] = w_ref[...]
        out_ref[peer, w_rows:, :] = slots[peer]


def split_halves(where, rows, new_rows, w_value, target, replicas):
    row_count, width = rows.shape
    w_rows, columns = w_value.shape
    steps = 4
    block = width // steps
    kept, sent = row_count + PAD, row_count // 2 + PAD
    return pl.pallas_call(
        halves_body,
        grid=(steps,),
        in_specs=[
            pl.BlockSpec(memory_space=pltpu.SMEM),
            pl.BlockSpec((row_count, block), lambda i: (0, i)),
            pl.BlockSpec((PAD, block), lambda i: (0, i)),
            pl.BlockSpec((w_rows, columns), lambda i: (0, 0)),
            pl.BlockSpec((row_count // steps, columns), lambda i: (i, 0)),
        ],
        out_specs=[
            pl.BlockSpec((kept, block // 2), lambda i: (0, i)),
            pl.BlockSpec((sent, block // 2), lambda i: (0, i)),
            pl.BlockSpec((replicas // steps, w_rows + SLOT, columns), lambda i: (i, 0, 0)),
        ],
        out_shape=[
            jax.ShapeDtypeStruct((kept, width // 2), BF16),
            jax.ShapeDtypeStruct((sent, width // 2), BF16),
            jax.ShapeDtypeStruct((replicas, w_rows + SLOT, columns), BF16),
        ],
        cost_estimate=pl.CostEstimate(
            flops=2 * (kept + sent) * width * LANES,
            bytes_accessed=4 * (row_count + PAD) * width,
            transcendentals=0,
        ),
        name="halves",
    )(where, rows, new_rows, w_value, target)


def partial_body(
    where_ref, kept_ref, first_ref, second_ref, block_ref, slot_ref, out_ref, new_ref, acc_ref
):
    step, last = pl.program_id(0), pl.num_programs(0) - 1
    core = where_ref[1]
    peers, block_rows, columns = block_ref.shape
    w_rows = block_rows - SLOT
    kept, half = kept_ref.shape[0], first_ref.shape[0] - PAD
    row_count = kept - PAD
    weights = block_ref[:, :w_rows, :].reshape(peers * w_rows, columns)
    slots = block_ref[:, w_rows:, :].reshape(peers * SLOT, columns)
    at = lax.broadcasted_iota(jnp.int32, (row_count, peers * SLOT), 0)
    place = one_hot(at == slot_ref[0])

    def times(rows):
        return jnp.dot(rows, weights, preferred_element_type=F32)

    kept_part = times(kept_ref[...])
    targets = jnp.dot(place, slots, preferred_element_type=F32)
    first_part = times(first_ref[...])
    second_part = times(second_ref[:half, :])
    keep_at, first_at = slice(0, kept), slice(kept, kept + half + PAD)
    second_at = slice(kept + half + PAD, kept + 2 * half + PAD)

    @pl.when(step == 0)
    def _():
        acc_ref[...] = jnp.zeros_like(acc_ref)

    acc_ref[keep_at, :] += kept_part
    acc_ref[:row_count, :] -= targets
    acc_ref[first_at, :] += first_part
    acc_ref[second_at, :] += second_part

    @pl.when(step == last)
    def _():
        out_ref[:row_count, :] = acc_ref[:row_count, :]
        near = pl.ds(pl.multiple_of(row_count + core * half, half), half)
        far = pl.ds(pl.multiple_of(row_count + (1 - core) * half, half), half)
        out_ref[near, :] = acc_ref[kept : kept + half, :]
        out_ref[far, :] = acc_ref[second_at, :]
        out_ref[2 * row_count :, :] = acc_ref[kept + half : kept + half + PAD, :]
        new_ref[...] = acc_ref[row_count:kept, :]


def partial_values(where, kept, first, second, arrived, slot_order):
    replicas, block_rows, columns = arrived.shape
    width = kept.shape[1]
    steps = 4
    block = width // steps
    kept_rows, first_rows = kept.shape[0], first.shape[0]
    row_count = kept_rows - PAD

    def rows_of(x):
        return pl.BlockSpec((x.shape[0], block), lambda i: (0, i))

    return pl.pallas_call(
        partial_body,
        grid=(steps,),
        in_specs=[
            pl.BlockSpec(memory_space=pltpu.SMEM),
            rows_of(kept),
            rows_of(first),
            rows_of(second),
            pl.BlockSpec((replicas // steps, block_rows, columns), lambda i: (i, 0, 0)),
            pl.BlockSpec((1, 1, replicas * SLOT // steps), lambda i: (i, 0, 0)),
        ],
        out_specs=[
            pl.BlockSpec((2 * row_count + PAD, columns), lambda i: (0, 0)),
            pl.BlockSpec((PAD, columns), lambda i: (0, 0)),
        ],
        out_shape=[
            jax.ShapeDtypeStruct((2 * row_count + PAD, columns), F32),
            jax.ShapeDtypeStruct((PAD, columns), F32),
        ],
        scratch_shapes=[pltpu.VMEM((kept_rows + first_rows + first_rows - PAD, columns), F32)],
        cost_estimate=pl.CostEstimate(
            flops=2 * width * columns * (kept_rows + 2 * first_rows),
            bytes_accessed=2 * width * (kept_rows + 2 * first_rows + columns),
            transcendentals=0,
        ),
        name="partial",
    )(where, kept, first, second, arrived, slot_order.reshape(steps, 1, -1))


def turn_body(kept_ref, first_ref, second_ref, out_ref):
    row_count = out_ref.shape[1] // 2
    half = row_count // 2
    out_ref[:, :row_count] = kept_ref[:row_count, :].T
    both = jnp.concatenate([first_ref[:half, :], second_ref[:half, :]], axis=0)
    out_ref[:, row_count:] = both.T


def turned(kept, first, second):
    width = kept.shape[1]
    steps = 4
    block = width // steps
    row_count = kept.shape[0] - PAD

    def rows_of(x):
        return pl.BlockSpec((x.shape[0], block), lambda i: (0, i))

    return pl.pallas_call(
        turn_body,
        grid=(steps,),
        in_specs=[rows_of(kept), rows_of(first), rows_of(second)],
        out_specs=pl.BlockSpec((block, 2 * row_count), lambda i: (i, 0)),
        out_shape=jax.ShapeDtypeStruct((width, 2 * row_count), BF16),
        cost_estimate=pl.CostEstimate(
            flops=0, bytes_accessed=8 * width * row_count, transcendentals=0
        ),
        name="turned",
    )(kept, first, second)


def product_body(where_ref, rows_ref, mine_ref, other_ref, out_ref):
    core = where_ref[1]
    row_count = rows_ref.shape[1] // 2
    half = row_count // 2

    def residual(at, its_at, size):
        return (mine_ref[pl.ds(at, size), :] + other_ref[pl.ds(its_at, size), :]).astype(BF16)

    near = pl.multiple_of(core * half, half)
    far = pl.multiple_of((1 - core) * half, half)
    own = residual(0, row_count, row_count)
    first = residual(row_count + near, near, half)
    second = residual(row_count + far, far, half)
    residuals = jnp.concatenate([own, first, second], axis=0)
    out_ref[...] = jnp.dot(rows_ref[...], residuals, preferred_element_type=F32).astype(BF16)


def weight_product(where, rows, mine, other):
    width, both = rows.shape
    columns = mine.shape[1]
    steps = 4
    block = width // steps
    return pl.pallas_call(
        product_body,
        grid=(steps,),
        in_specs=[
            pl.BlockSpec(memory_space=pltpu.SMEM),
            pl.BlockSpec((block, both), lambda i: (i, 0)),
            pl.BlockSpec(mine.shape, lambda i: (0, 0)),
            pl.BlockSpec(other.shape, lambda i: (0, 0)),
        ],
        out_specs=pl.BlockSpec((block, columns), lambda i: (i, 0)),
        out_shape=jax.ShapeDtypeStruct((width, columns), BF16),
        cost_estimate=pl.CostEstimate(
            flops=2 * width * columns * both,
            bytes_accessed=2 * width * (both + columns),
            transcendentals=0,
        ),
        name="product",
    )(where, rows, mine, other)


def swap_section(x):
    return lax.ppermute(x, "section", [(0, 1), (1, 0)])


def swap_core(x):
    return lax.ppermute(x, "tensor", [(i, i ^ 1) for i in range(lax.axis_size("tensor"))])


def per_device(
    w_value,
    hidden_new,
    query,
    key_new,
    key_cache,
    value_cache,
    cache_len,
    sampled_rows,
    mb_map,
    value_target,
):
    replicas = lax.axis_size(DP)
    section = lax.axis_index("section")
    core = lax.axis_index("tensor") % 2
    row_count = sampled_rows.shape[0]
    per_peer = row_count // replicas
    w_rows, width_local = w_value.shape
    prompts = hidden_new.shape[0]
    new_count = prompts * NEW
    new_rows = hidden_new.reshape(new_count, hidden_new.shape[2])
    new_rows = jnp.pad(new_rows, ((0, PAD - new_count), (0, 0)))
    slot_order = jnp.pad(
        mb_map[0].reshape(replicas, per_peer), ((0, 0), (0, SLOT - per_peer)), constant_values=-1
    )

    where = jnp.stack([section, core]).astype(jnp.int32)
    kept, sent, outgoing = split_halves(
        where, sampled_rows, new_rows, w_value, value_target, replicas
    )
    first = swap_section(sent)
    arrived = lax.all_to_all(outgoing, DP, 0, 0, tiled=True)
    second = swap_core(first)
    partial, new_part = partial_values(where, kept, first, second, arrived, slot_order)
    other = swap_section(partial)
    rows_turned = turned(kept, first, second)
    v_new_rows = (new_part + other[2 * row_count :])[:new_count]
    product = weight_product(where, rows_turned, partial, other)
    terms = lax.all_to_all(
        product.reshape(replicas, w_rows, width_local), DP, 0, 0, tiled=True
    )
    grad_value = jnp.sum(terms.astype(jnp.float32), axis=0) / row_count
    heads_local = width_local // HD
    cache_size = key_cache.shape[1]
    scale = 1.0 / jnp.sqrt(jnp.float32(HD))
    v_new = v_new_rows.astype(jnp.bfloat16).reshape(prompts, NEW, heads_local, HD)
    query_h = query.reshape(prompts, NEW, heads_local, QPK, HD)
    kc_heads = key_cache.reshape(prompts, cache_size, heads_local, HD)
    vc_heads = value_cache.reshape(prompts, cache_size, heads_local, HD)
    kn_heads = key_new.reshape(prompts, NEW, heads_local, HD)
    score_cache = (
        jnp.einsum("ptgqd,pjgd->pgtqj", query_h, kc_heads, preferred_element_type=jnp.float32)
        * scale
    )
    score_new = (
        jnp.einsum("ptgqd,pugd->pgtqu", query_h, kn_heads, preferred_element_type=jnp.float32)
        * scale
    )
    live_cache = (jnp.arange(cache_size)[None, :] < cache_len[:, None])[:, None, None, None, :]
    live_new = (jnp.arange(NEW)[None, :] <= jnp.arange(NEW)[:, None])[None, None, :, None, :]
    score_cache = jnp.where(live_cache, score_cache, -1e30)
    score_new = jnp.where(live_new, score_new, -1e30)
    peak = jnp.maximum(jnp.max(score_cache, axis=-1), jnp.max(score_new, axis=-1))[..., None]
    exp_cache = jnp.where(live_cache, jnp.exp(score_cache - peak), 0.0)
    exp_new = jnp.where(live_new, jnp.exp(score_new - peak), 0.0)
    total = jnp.sum(exp_cache, axis=-1, keepdims=True) + jnp.sum(exp_new, axis=-1, keepdims=True)
    prob_cache = (exp_cache / total).astype(jnp.bfloat16)
    prob_new = (exp_new / total).astype(jnp.bfloat16)
    mixed = jnp.einsum(
        "pgtqj,pjgd->ptgqd", prob_cache, vc_heads, preferred_element_type=jnp.float32
    )
    mixed = mixed + jnp.einsum(
        "pgtqu,pugd->ptgqd", prob_new, v_new, preferred_element_type=jnp.float32
    )
    attn_out = mixed.reshape(prompts, NEW, heads_local * QPK * HD).astype(jnp.bfloat16)
    return (attn_out, grad_value)


def solution(mesh):
    torus = Mesh(
        mesh.devices.reshape(8, 8, mesh.shape["tensor"], mesh.shape["section"]),
        ("dp_0", "dp_1", "tensor", "section"),
    )
    return jax.shard_map(
        per_device,
        mesh=torus,
        in_specs=(
            P(DP_SECTION, "tensor"),
            P(DP_SECTION, None, None),
            P(DP_SECTION, None, "tensor"),
            P(DP_SECTION, None, "tensor"),
            P(DP_SECTION, None, "tensor"),
            P(DP_SECTION, None, "tensor"),
            P(DP_SECTION),
            P(DP_SECTION, None),
            P(DP_SECTION, None),
            P(DP_SECTION, "tensor"),
        ),
        out_specs=(P(DP_SECTION, None, "tensor"), P(DP_SECTION, "tensor")),
        check_vma=False,
    )
```

time: 136 us -> 136 us (level)
  Pallas kernels: 9.17 us -> 17.5 us
  waiting for transfers between devices: 45.1 us -> 40.2 us
  other arithmetic: 5.07 us -> 2.57 us
  matrix products: 5.37 us -> 3.77 us
  local copies, waits for them, and re-layouts: 4.79 us -> 6.25 us
    pallas_call x2 -> x4, Pallas kernels: 9.17 us -> 17.5 us  [the longest x1 5 us: split_halves(): pl.pallas_call(halves_body, grid=(steps,), in_specs=[pl.BlockSpec(memory_...]
    ppermute x2, waiting for transfers between devices: 18.9 us -> 14.5 us  [swap_section(): return lax.ppermute(x, 'section', [(0, 1), (1, 0)])]
    dot_general x4 -> x0, matrix products: 2.32 us -> none  [the longest x3 2.19 us: times(): return jnp.dot(rows, piece, preferred_element_type=jnp.float32)]
    slice x6 -> x2, local copies, waits for them, and re-layouts: 2.23 us -> 0.01 us  [per_device(): v_new_rows = (new_part + other[2 * row_count:])[:new_count]]
    unnamed x18 -> x19, local copies, waits for them, and re-layouts: 0.05 us -> 2.22 us
    concatenate x2 -> x0, other arithmetic: 1.91 us -> none  [the longest x1 1.89 us: per_device(): jnp.concatenate([jnp.broadcast_to(w_value[None], (replicas, w_rows, width...]
  transfers between devices with their start and end apart: 5 -> 5, of which waited for: 3 -> 3; matrix products, arithmetic and copies ran while one was open for 7% -> 6% of each run, Pallas kernels for 4% -> 3%
where the time goes in v3:
time: 136 us
  starting transfers between devices  64.4 us (47%)
  waiting for transfers between devices  40.2 us (30%)
  Pallas kernels  17.5 us (13%)
  local copies, waits for them, and re-layouts  6.25 us (5%)
  matrix products  3.77 us (3%)
  other arithmetic  2.57 us (2%)
    ppermute x2, starting transfers between devices, swap_section(): return lax.ppermute(x, 'section', [(0, 1), (1, 0)])  32.2 us
    all_to_all x1, waiting for transfers between devices, per_device(): lax.all_to_all(product.reshape(replicas, w_rows, width_local), DP, 0, 0,...  25.5 us
    all_to_all x1, starting transfers between devices, per_device(): arrived = lax.all_to_all(outgoing, DP, 0, 0, tiled=True)  17.5 us
    ppermute x2, waiting for transfers between devices, swap_section(): return lax.ppermute(x, 'section', [(0, 1), (1, 0)])  14.5 us
    all_to_all x1, starting transfers between devices, per_device(): lax.all_to_all(product.reshape(replicas, w_rows, width_local), DP, 0, 0,...  12.8 us
    pallas_call x1, Pallas kernels, split_halves(): pl.pallas_call(halves_body, grid=(steps,), in_specs=[pl.BlockSpec(memory_...  5 us
    pallas_call x1, Pallas kernels, weight_product(): pl.pallas_call(product_body, grid=(steps,), in_specs=[pl.BlockSpec(memory...  4.25 us
    pallas_call x1, Pallas kernels, turned(): pl.pallas_call(turn_body, grid=(steps,), in_specs=[rows_of(kept), rows_of...  4.17 us
  transfers between devices with their start and end apart: 5, of which 3 were waited for; matrix products, arithmetic and copies ran while one was open for 6% of the time, Pallas kernels for 3%

profile of v3, /device:TPU:4, one launch (start us, length us, event | category | flops | bytes accessed | tf_op | source)
XLA Modules:
  0.0 135.6 jit_solution(14858967547126235085)
XLA Ops:
  0.6 0.0 copy-start
  0.7 1.1 reshape.128
  1.8 0.6 pad_add_fusion.where_ref
  2.4 0.7 pad.8.new_ref
  3.1 5.0 %halves.1 = (bf16[144,4096]{1,0:T(8,128)(2,1)}, bf16[80,4096]{1,0:T(8,128)(2,1)}, bf16[64,72,128]{2,1,0:T(8,128)(2,1)}) custom-call(s32[2]{0:T(128)} %pad_add_fusion.where_ref, bf16[128,8192]{1,0:T(8,128)(2,1)} %rows_ref.1, bf16[16,8192]{1,0:T(8,128)(2,1)} %pad.8.new_ref, bf16[64,128]{1,0:T(8,128)(2,1)} %w_ref.1, bf16[128,128]{1,0:T(8,128)(2,1)} %target_ref.1), custom_call_target="tpu_custom_call" | custom-call | flops 469762048 | bytes 4718592 | tf_op jit(solution)/shard_map/halves/pallas_call | solution.py:69
  8.1 0.0 copy-start.8
  8.1 17.5 %all-to-all-start = ((bf16[64,72,128]{2,1,0:T(8,128)(2,1)}), bf16[64,72,128]{2,1,0:T(8,128)(2,1)S(1)}, u32[]{:S(2)}, u32[]{:S(2)}) async-start(bf16[64,72,128]{2,1,0:T(8,128)(2,1)} %get-tuple-element.9), calls=%async_computation | async-start | bytes 2359296 | tf_op jit(solution)/shard_map/all_to_all | solution.py:293
  25.6 10.8 %collective-permute-start = (bf16[80,4096]{1,0:T(8,128)(2,1)}, bf16[80,4096]{1,0:T(8,128)(2,1)S(1)}, u32[]{:S(2)}, u32[]{:S(2)}) collective-permute-start(bf16[80,4096]{1,0:T(8,128)(2,1)} %get-tuple-element.8), channel_id=1, source_target_pairs={{0,1},{1,0},{2,3},{3,2},{4,5},{5,4},{6,7},{7,6},{8,9},{9,8},{10,11... | collective-permute-start | bytes 1966088 | tf_op jit(solution)/shard_map/ppermute | solution.py:255
  36.3 14.5 %collective-permute-done.first_ref = bf16[80,4096]{1,0:T(8,128)(2,1)S(1)} collective-permute-done((bf16[80,4096]{1,0:T(8,128)(2,1)}, bf16[80,4096]{1,0:T(8,128)(2,1)S(1)}, u32[]{:S(2)}, u32[]{:S(2)}) %collective-permute-start) | collective-permute-done | bytes 655392 | tf_op jit(solution)/shard_map/ppermute | solution.py:255
  50.9 0.0 copy-start.2
  50.9 1.9 %collective-permute-start.1 = (bf16[80,4096]{1,0:T(8,128)(2,1)S(1)}, bf16[80,4096]{1,0:T(8,128)(2,1)}, u32[]{:S(2)}, u32[]{:S(2)}) collective-permute-start(bf16[80,4096]{1,0:T(8,128)(2,1)S(1)} %collective-permute-done.first_ref), channel_id=1, source_target_pairs={{0,2},{2,0},{4,6},{6,4},{8,10},{10,8},{12,14},{14,12},{1,3},{3,1},... | collective-permute-start | bytes 1966088 | tf_op jit(solution)/shard_map/ppermute | solution.py:259
  52.8 0.5 broadcast.43
  53.3 0.0 copy-done.8
  53.3 0.7 reduce.11
  54.0 0.1 reshape_squeeze.3
  54.1 0.7 reshape.129
  54.8 0.2 collective-permute-done.1.second_ref
  55.0 0.0 all-to-all-done.block_ref
  55.0 0.0 copy-start.1
  55.0 0.0 copy-done.2
  55.0 1.0 copy-done.1
  56.0 4.1 %partial.1 = (f32[272,128]{1,0:T(8,128)}, f32[16,128]{1,0:T(8,128)}) custom-call(s32[2]{0:T(128)} %pad_add_fusion.where_ref, bf16[144,4096]{1,0:T(8,128)(2,1)} %get-tuple-element.7.kept_ref, bf16[80,4096]{1,0:T(8,128)(2,1)} %copy-done.2, bf16[80,4096]{1,0:T(8,128)(2,1)} %collective-permute-done.1.second_ref, bf16[64,72,128]{2,1,0:T(8,128)(2,1)} %copy-done.1, ...), custom_call_target="tpu_custom_call" | custom-call | flops 318767104 | bytes 3538944 | tf_op jit(solution)/shard_map/partial/pallas_call | solution.py:153
  60.1 21.4 %collective-permute-start.2 = (f32[272,128]{1,0:T(8,128)}, f32[272,128]{1,0:T(8,128)S(1)}, u32[]{:S(2)}, u32[]{:S(2)}) collective-permute-start(f32[272,128]{1,0:T(8,128)} %get-tuple-element.11.mine_ref), channel_id=1, source_target_pairs={{0,1},{1,0},{2,3},{3,2},{4,5},{5,4},{6,7},{7,6},{8,9},{9,8},{10,11... | collective-permute-start | bytes 417800 | tf_op jit(solution)/shard_map/ppermute | solution.py:255
  81.6 0.8 reshape.127
  82.3 0.0 copy-start.4
  82.4 4.2 %turned.1.rows_ref = bf16[4096,256]{1,0:T(8,128)(2,1)} custom-call(bf16[144,4096]{1,0:T(8,128)(2,1)} %get-tuple-element.7.kept_ref, bf16[80,4096]{1,0:T(8,128)(2,1)} %copy-done.2, bf16[80,4096]{1,0:T(8,128)(2,1)} %collective-permute-done.1.second_ref), custom_call_target="tpu_custom_call" | custom-call | bytes 4194304 | tf_op jit(solution)/shard_map/turned/pallas_call | solution.py:199
  86.5 0.0 collective-permute-done.2.other_ref
  86.5 0.0 copy-start.3
  86.5 0.7 copy-done.3
  87.2 4.2 %product.1 = bf16[4096,128]{1,0:T(8,128)(2,1)} custom-call(s32[2]{0:T(128)} %pad_add_fusion.where_ref, bf16[4096,256]{1,0:T(8,128)(2,1)} %turned.1.rows_ref, f32[272,128]{1,0:T(8,128)} %get-tuple-element.11.mine_ref, f32[272,128]{1,0:T(8,128)} %copy-done.3), custom_call_target="tpu_custom_call" | custom-call | flops 268435456 | bytes 3145728 | tf_op jit(solution)/shard_map/product/pallas_call | solution.py:234
  91.4 0.0 copy-start.7
  91.4 0.0 copy-start.6
  91.4 12.8 %all-to-all-start.1 = ((bf16[64,64,128]{2,1,0:T(8,128)(2,1)}), bf16[64,64,128]{2,1,0:T(8,128)(2,1)S(1)}, u32[]{:S(2)}, u32[]{:S(2)}) async-start(bf16[64,64,128]{2,1,0:T(8,128)(2,1)} %bitcast.52), calls=%async_computation.1 | async-start | bytes 2097152 | tf_op jit(solution)/shard_map/all_to_all | solution.py:300
  104.3 0.0 copy-done.4
  104.3 0.0 copy-done.7
  104.3 0.2 fusion.34
  104.5 0.0 copy-done.6
  104.6 0.1 iota_compare_fusion
  104.6 0.0 copy-done
  104.6 0.0 slice-start
  104.7 0.0 copy-start.5
  104.7 1.4 %fusion.33 = (f32[3,4,8]{2,1,0:T(4,128)S(1)}, f32[3,4,8,2048]{3,2,1,0:T(8,128)S(1)}) fusion(bf16[3,4,8,128]{3,2,1,0:T(8,128)(2,1)} %copy-done.4, bf16[3,2048,128]{2,1,0:T(8,128)(2,1)S(1)} %copy-done, pred[3,2048]{1,0:T(4,128)(4,1)S(1)} %iota_compare_fusion), kind=kOutput, calls=%fused_computation.37 | convolution fusion | flops 50921376 | bytes 2390400 | tf_op jit(solution)/shard_map/ptgqd,pjgd->pgtqj/dot_general | solution.py:313
  106.1 0.1 fusion.22
  106.2 0.3 fusion.17
  106.5 0.0 slice-done
  106.5 0.0 copy-done.5
  106.6 0.3 fusion.23
  106.8 1.8 %fusion.13 = bf16[3,4,1,8,128]{4,3,1,0,2:T(8,128)(2,1)S(1)} fusion(f32[3,128,4,8]{1,3,2,0:T(8,128)S(1)} %fusion.23, bf16[3,2048,128]{2,1,0:T(8,128)(2,1)} %param.15, f32[3,4,8,2048]{3,2,1,0:T(8,128)S(1)} %get-tuple-element.13, f32[3,4,8]{2,1,0:T(4,128)S(1)} %add.24, f32[3,4,8]{2,1,0:T(4,128)S(1)} %max.9, pred[3,2048]{1,0:T(4,128)(4,1)S(1)} %iota_compare_fusion), kind=kOutput, calls=%fused_computation.9 | convolution fusion | flops 51142656 | bytes 2439936 | tf_op jit(solution)/shard_map/pgtqj,pjgd->ptgqd/dot_general | solution.py:330
  108.7 0.6 convert_element_type.31
  109.3 25.5 %all-to-all-done.1 = bf16[64,64,128]{2,1,0:T(8,128)(2,1)S(1)} async-done(((bf16[64,64,128]{2,1,0:T(8,128)(2,1)}), bf16[64,64,128]{2,1,0:T(8,128)(2,1)S(1)}, u32[]{:S(2)}, u32[]{:S(2)}) %all-to-all-start.1) | async-done | bytes 1048608 | tf_op jit(solution)/shard_map/all_to_all | solution.py:300
  134.8 0.2 convert_reduce_fusion
  134.9 0.6 broadcast_multiply_fusion
  (6 shorter events, 0.0 us)
Async XLA Ops:
  0.6 104.0 %copy-start = (bf16[3,2048,128]{2,1,0:T(8,128)(2,1)S(1)}, bf16[3,2048,128]{2,1,0:T(8,128)(2,1)}, u32[]{:S(2)}) copy-start(bf16[3,2048,128]{2,1,0:T(8,128)(2,1)} %param.14) | copy-start | bytes 4718596
  8.1 45.2 %copy-start.8 = (s32[1,128]{1,0:T(1,128)S(1)}, s32[1,128]{1,0:T(1,128)}, u32[]{:S(2)}) copy-start(s32[1,128]{1,0:T(1,128)} %param.18) | copy-start | bytes 1540
  8.1 46.9 %all-to-all-start = ((bf16[64,72,128]{2,1,0:T(8,128)(2,1)}), bf16[64,72,128]{2,1,0:T(8,128)(2,1)S(1)}, u32[]{:S(2)}, u32[]{:S(2)}) async-start(bf16[64,72,128]{2,1,0:T(8,128)(2,1)} %get-tuple-element.9), calls=%async_computation | async-start | bytes 2359296 | tf_op jit(solution)/shard_map/all_to_all | solution.py:293
  25.6 25.3 %collective-permute-start = (bf16[80,4096]{1,0:T(8,128)(2,1)}, bf16[80,4096]{1,0:T(8,128)(2,1)S(1)}, u32[]{:S(2)}, u32[]{:S(2)}) collective-permute-start(bf16[80,4096]{1,0:T(8,128)(2,1)} %get-tuple-element.8), channel_id=1, source_target_pairs={{0,1},{1,0},{2,3},{3,2},{4,5},{5,4},{6,7},{7,6},{8,9},{9,8},{10,11... | collective-permute-start | bytes 1966088 | tf_op jit(solution)/shard_map/ppermute | solution.py:255
  50.9 4.1 %copy-start.2 = (bf16[80,4096]{1,0:T(8,128)(2,1)}, bf16[80,4096]{1,0:T(8,128)(2,1)S(1)}, u32[]{:S(2)}) copy-start(bf16[80,4096]{1,0:T(8,128)(2,1)S(1)} %collective-permute-done.first_ref) | copy-start | bytes 1966084
  50.9 4.1 %collective-permute-start.1 = (bf16[80,4096]{1,0:T(8,128)(2,1)S(1)}, bf16[80,4096]{1,0:T(8,128)(2,1)}, u32[]{:S(2)}, u32[]{:S(2)}) collective-permute-start(bf16[80,4096]{1,0:T(8,128)(2,1)S(1)} %collective-permute-done.first_ref), channel_id=1, source_target_pairs={{0,2},{2,0},{4,6},{6,4},{8,10},{10,8},{12,14},{14,12},{1,3},{3,1},... | collective-permute-start | bytes 1966088 | tf_op jit(solution)/shard_map/ppermute | solution.py:259
  55.0 1.0 copy-start.1
  60.1 26.4 %collective-permute-start.2 = (f32[272,128]{1,0:T(8,128)}, f32[272,128]{1,0:T(8,128)S(1)}, u32[]{:S(2)}, u32[]{:S(2)}) collective-permute-start(f32[272,128]{1,0:T(8,128)} %get-tuple-element.11.mine_ref), channel_id=1, source_target_pairs={{0,1},{1,0},{2,3},{3,2},{4,5},{5,4},{6,7},{7,6},{8,9},{9,8},{10,11... | collective-permute-start | bytes 417800 | tf_op jit(solution)/shard_map/ppermute | solution.py:255
  82.3 21.9 %copy-start.4 = (bf16[3,4,8,128]{3,2,1,0:T(8,128)(2,1)}, bf16[3,4,8,128]{3,2,1,0:T(8,128)(2,1)S(1)}, u32[]{:S(2)}) copy-start(bf16[3,4,8,128]{3,2,1,0:T(8,128)(2,1)S(1)} %reshape.127) | copy-start | bytes 73732
  86.5 0.7 copy-start.3
  91.4 12.9 %copy-start.7 = (bf16[3,4,128]{2,1,0:T(4,128)(2,1)S(1)}, bf16[3,4,128]{2,1,0:T(4,128)(2,1)}, u32[]{:S(2)}) copy-start(bf16[3,4,128]{2,1,0:T(4,128)(2,1)} %param.13) | copy-start | bytes 9220
  91.4 13.1 %copy-start.6 = (s32[3]{0:T(128)S(1)}, s32[3]{0:T(128)}, u32[]{:S(2)}) copy-start(s32[3]{0:T(128)} %param.16) | copy-start | bytes 40
  91.4 43.3 %all-to-all-start.1 = ((bf16[64,64,128]{2,1,0:T(8,128)(2,1)}), bf16[64,64,128]{2,1,0:T(8,128)(2,1)S(1)}, u32[]{:S(2)}, u32[]{:S(2)}) async-start(bf16[64,64,128]{2,1,0:T(8,128)(2,1)} %bitcast.52), calls=%async_computation.1 | async-start | bytes 2097152 | tf_op jit(solution)/shard_map/all_to_all | solution.py:300
  104.6 1.9 %slice-start = ((f32[272,128]{1,0:T(8,128)}), f32[16,128]{1,0:T(8,128)S(1)}, s32[]{:S(2)}) async-start(f32[272,128]{1,0:T(8,128)} %copy-done.3), calls=%async_computation.2 | async-start | bytes 16384 | tf_op jit(solution)/shard_map/slice | solution.py:298
  104.7 1.9 %copy-start.5 = (f32[16,128]{1,0:T(8,128)S(1)}, f32[16,128]{1,0:T(8,128)}, u32[]{:S(2)}) copy-start(f32[16,128]{1,0:T(8,128)} %get-tuple-element.10) | copy-start | bytes 24580

commit v4 on v3

--- a/solution.py
+++ b/solution.py
@@ -12,6 +12,7 @@
 LANES = 128
 PAD = 16
 SLOT = 8
+GRANT = 20 * 1024 * 1024
 DP = ("dp_0", "dp_1")
 DP_SECTION = ("dp_0", "dp_1", "section")
 F32, BF16 = jnp.float32, jnp.bfloat16
@@ -28,8 +29,12 @@
     return one_hot(row == source)
 
 
-def halves_body(where_ref, rows_ref, new_ref, w_ref, target_ref, keep_ref, send_ref, out_ref):
-    section, core = where_ref[0], where_ref[1]
+def core_index():
+    return lax.axis_index("tensor") % 2
+
+
+def halves_body(rows_ref, new_ref, w_ref, target_ref, keep_ref, send_ref, out_ref, new_scr):
+    section, core = lax.axis_index("section"), core_index()
     row_count = rows_ref.shape[0]
     half = row_count // 2
     w_rows = w_ref.shape[0]
@@ -37,6 +42,11 @@
     own = picker(section, w_rows)
     other = picker(1 - section, w_rows)
 
+    prompts, new, _ = new_ref.shape
+    new_scr[...] = jnp.zeros_like(new_scr)
+    for prompt in range(prompts):
+        new_scr[prompt * new : (prompt + 1) * new, :] = new_ref[prompt].astype(F32)
+
     def pick(block, which):
         return jnp.dot(block, which, preferred_element_type=F32).astype(BF16)
 
@@ -44,9 +54,10 @@
         wide = slice(tile * 2 * LANES, (tile + 1) * 2 * LANES)
         thin = slice(tile * LANES, (tile + 1) * LANES)
         keep_ref[:row_count, thin] = pick(rows_ref[:, wide], own)
-        keep_ref[row_count:, thin] = pick(new_ref[:, wide], own)
+        fresh = new_scr[:, wide].astype(BF16)
+        keep_ref[row_count:, thin] = pick(fresh, own)
         send_ref[:half, thin] = pick(rows_ref[sent_at, wide], other)
-        send_ref[half:, thin] = pick(new_ref[:, wide], other)
+        send_ref[half:, thin] = pick(fresh, other)
     peers = out_ref.shape[0]
     targets = target_ref.shape[0]
     per_peer = targets // peers
@@ -60,7 +71,7 @@
         out_ref[peer, w_rows:, :] = slots[peer]
 
 
-def split_halves(where, rows, new_rows, w_value, target, replicas):
+def split_halves(rows, new_rows, w_value, target, replicas):
     row_count, width = rows.shape
     w_rows, columns = w_value.shape
     steps = 4
@@ -70,9 +81,8 @@
         halves_body,
         grid=(steps,),
         in_specs=[
-            pl.BlockSpec(memory_space=pltpu.SMEM),
             pl.BlockSpec((row_count, block), lambda i: (0, i)),
-            pl.BlockSpec((PAD, block), lambda i: (0, i)),
+            pl.BlockSpec((*new_rows.shape[:2], block), lambda i: (0, 0, i)),
             pl.BlockSpec((w_rows, columns), lambda i: (0, 0)),
             pl.BlockSpec((row_count // steps, columns), lambda i: (i, 0)),
         ],
@@ -91,15 +101,18 @@
             bytes_accessed=4 * (row_count + PAD) * width,
             transcendentals=0,
         ),
+        scratch_shapes=[pltpu.VMEM((PAD, block), F32)],
         name="halves",
-    )(where, rows, new_rows, w_value, target)
+    )(rows, new_rows, w_value, target)
+
+
+VMEM = pl.BlockSpec(memory_space=pltpu.VMEM)
 
 
 def partial_body(
-    where_ref, kept_ref, first_ref, second_ref, block_ref, slot_ref, out_ref, new_ref, acc_ref
+    kept_ref, first_ref, second_ref, block_ref, slot_ref, out_ref, new_ref
 ):
-    step, last = pl.program_id(0), pl.num_programs(0) - 1
-    core = where_ref[1]
+    core = core_index()
     peers, block_rows, columns = block_ref.shape
     w_rows = block_rows - SLOT
     kept, half = kept_ref.shape[0], first_ref.shape[0] - PAD
@@ -107,110 +120,77 @@
     weights = block_ref[:, :w_rows, :].reshape(peers * w_rows, columns)
     slots = block_ref[:, w_rows:, :].reshape(peers * SLOT, columns)
     at = lax.broadcasted_iota(jnp.int32, (row_count, peers * SLOT), 0)
-    place = one_hot(at == slot_ref[0])
+    place = one_hot(at == slot_ref[...])
+    targets = jnp.dot(place, slots, preferred_element_type=F32)
 
     def times(rows):
         return jnp.dot(rows, weights, preferred_element_type=F32)
 
     kept_part = times(kept_ref[...])
-    targets = jnp.dot(place, slots, preferred_element_type=F32)
     first_part = times(first_ref[...])
     second_part = times(second_ref[:half, :])
-    keep_at, first_at = slice(0, kept), slice(kept, kept + half + PAD)
-    second_at = slice(kept + half + PAD, kept + 2 * half + PAD)
-
-    @pl.when(step == 0)
-    def _():
-        acc_ref[...] = jnp.zeros_like(acc_ref)
-
-    acc_ref[keep_at, :] += kept_part
-    acc_ref[:row_count, :] -= targets
-    acc_ref[first_at, :] += first_part
-    acc_ref[second_at, :] += second_part
-
-    @pl.when(step == last)
-    def _():
-        out_ref[:row_count, :] = acc_ref[:row_count, :]
-        near = pl.ds(pl.multiple_of(row_count + core * half, half), half)
-        far = pl.ds(pl.multiple_of(row_count + (1 - core) * half, half), half)
-        out_ref[near, :] = acc_ref[kept : kept + half, :]
-        out_ref[far, :] = acc_ref[second_at, :]
-        out_ref[2 * row_count :, :] = acc_ref[kept + half : kept + half + PAD, :]
-        new_ref[...] = acc_ref[row_count:kept, :]
-
-
-def partial_values(where, kept, first, second, arrived, slot_order):
-    replicas, block_rows, columns = arrived.shape
+    near = pl.ds(pl.multiple_of(row_count + core * half, half), half)
+    far = pl.ds(pl.multiple_of(row_count + (1 - core) * half, half), half)
+    out_ref[:row_count, :] = kept_part[:row_count] - targets
+    out_ref[near, :] = first_part[:half]
+    out_ref[far, :] = second_part
+    out_ref[2 * row_count :, :] = first_part[half:]
+    new_ref[...] = kept_part[row_count:]
+
+
+def partial_values(kept, first, second, arrived, slot_order):
+    columns = arrived.shape[2]
     width = kept.shape[1]
-    steps = 4
-    block = width // steps
-    kept_rows, first_rows = kept.shape[0], first.shape[0]
-    row_count = kept_rows - PAD
-
-    def rows_of(x):
-        return pl.BlockSpec((x.shape[0], block), lambda i: (0, i))
-
+    row_count = kept.shape[0] - PAD
+    rows = kept.shape[0] + 2 * first.shape[0]
     return pl.pallas_call(
         partial_body,
-        grid=(steps,),
-        in_specs=[
-            pl.BlockSpec(memory_space=pltpu.SMEM),
-            rows_of(kept),
-            rows_of(first),
-            rows_of(second),
-            pl.BlockSpec((replicas // steps, block_rows, columns), lambda i: (i, 0, 0)),
-            pl.BlockSpec((1, 1, replicas * SLOT // steps), lambda i: (i, 0, 0)),
-        ],
-        out_specs=[
-            pl.BlockSpec((2 * row_count + PAD, columns), lambda i: (0, 0)),
-            pl.BlockSpec((PAD, columns), lambda i: (0, 0)),
-        ],
+        in_specs=[VMEM] * 5,
+        out_specs=[VMEM, VMEM],
         out_shape=[
             jax.ShapeDtypeStruct((2 * row_count + PAD, columns), F32),
             jax.ShapeDtypeStruct((PAD, columns), F32),
         ],
-        scratch_shapes=[pltpu.VMEM((kept_rows + first_rows + first_rows - PAD, columns), F32)],
         cost_estimate=pl.CostEstimate(
-            flops=2 * width * columns * (kept_rows + 2 * first_rows),
-            bytes_accessed=2 * width * (kept_rows + 2 * first_rows + columns),
+            flops=2 * width * columns * rows,
+            bytes_accessed=2 * width * (rows + columns),
             transcendentals=0,
         ),
+        compiler_params=pltpu.CompilerParams(vmem_limit_bytes=GRANT),
         name="partial",
-    )(where, kept, first, second, arrived, slot_order.reshape(steps, 1, -1))
+    )(kept, first, second, arrived, slot_order.reshape(1, -1))
 
 
 def turn_body(kept_ref, first_ref, second_ref, out_ref):
-    row_count = out_ref.shape[1] // 2
+    width, both = out_ref.shape
+    row_count = both // 2
     half = row_count // 2
-    out_ref[:, :row_count] = kept_ref[:row_count, :].T
-    both = jnp.concatenate([first_ref[:half, :], second_ref[:half, :]], axis=0)
-    out_ref[:, row_count:] = both.T
+    block = 512
+    for start in range(0, width, block):
+        at = slice(start, start + block)
+        out_ref[at, :row_count] = kept_ref[:row_count, at].T
+        pair = jnp.concatenate([first_ref[:half, at], second_ref[:half, at]], axis=0)
+        out_ref[at, row_count:] = pair.T
 
 
 def turned(kept, first, second):
     width = kept.shape[1]
-    steps = 4
-    block = width // steps
     row_count = kept.shape[0] - PAD
-
-    def rows_of(x):
-        return pl.BlockSpec((x.shape[0], block), lambda i: (0, i))
-
     return pl.pallas_call(
         turn_body,
-        grid=(steps,),
-        in_specs=[rows_of(kept), rows_of(first), rows_of(second)],
-        out_specs=pl.BlockSpec((block, 2 * row_count), lambda i: (i, 0)),
+        in_specs=[VMEM, VMEM, VMEM],
+        out_specs=VMEM,
         out_shape=jax.ShapeDtypeStruct((width, 2 * row_count), BF16),
         cost_estimate=pl.CostEstimate(
             flops=0, bytes_accessed=8 * width * row_count, transcendentals=0
         ),
+        compiler_params=pltpu.CompilerParams(vmem_limit_bytes=GRANT),
         name="turned",
     )(kept, first, second)
 
 
-def product_body(where_ref, rows_ref, mine_ref, other_ref, out_ref):
-    core = where_ref[1]
+def product_body(rows_ref, mine_ref, other_ref, out_ref):
+    core = core_index()
     row_count = rows_ref.shape[1] // 2
     half = row_count // 2
 
@@ -226,29 +206,22 @@
     out_ref[...] = jnp.dot(rows_ref[...], residuals, preferred_element_type=F32).astype(BF16)
 
 
-def weight_product(where, rows, mine, other):
+def weight_product(rows, mine, other):
     width, both = rows.shape
     columns = mine.shape[1]
-    steps = 4
-    block = width // steps
     return pl.pallas_call(
         product_body,
-        grid=(steps,),
-        in_specs=[
-            pl.BlockSpec(memory_space=pltpu.SMEM),
-            pl.BlockSpec((block, both), lambda i: (i, 0)),
-            pl.BlockSpec(mine.shape, lambda i: (0, 0)),
-            pl.BlockSpec(other.shape, lambda i: (0, 0)),
-        ],
-        out_specs=pl.BlockSpec((block, columns), lambda i: (i, 0)),
+        in_specs=[VMEM] * 3,
+        out_specs=VMEM,
         out_shape=jax.ShapeDtypeStruct((width, columns), BF16),
         cost_estimate=pl.CostEstimate(
             flops=2 * width * columns * both,
             bytes_accessed=2 * width * (both + columns),
             transcendentals=0,
         ),
+        compiler_params=pltpu.CompilerParams(vmem_limit_bytes=GRANT),
         name="product",
-    )(where, rows, mine, other)
+    )(rows, mine, other)
 
 
 def swap_section(x):
@@ -272,31 +245,26 @@
     value_target,
 ):
     replicas = lax.axis_size(DP)
-    section = lax.axis_index("section")
-    core = lax.axis_index("tensor") % 2
     row_count = sampled_rows.shape[0]
     per_peer = row_count // replicas
     w_rows, width_local = w_value.shape
     prompts = hidden_new.shape[0]
     new_count = prompts * NEW
-    new_rows = hidden_new.reshape(new_count, hidden_new.shape[2])
-    new_rows = jnp.pad(new_rows, ((0, PAD - new_count), (0, 0)))
     slot_order = jnp.pad(
         mb_map[0].reshape(replicas, per_peer), ((0, 0), (0, SLOT - per_peer)), constant_values=-1
     )
 
-    where = jnp.stack([section, core]).astype(jnp.int32)
     kept, sent, outgoing = split_halves(
-        where, sampled_rows, new_rows, w_value, value_target, replicas
+        sampled_rows, hidden_new, w_value, value_target, replicas
     )
     first = swap_section(sent)
     arrived = lax.all_to_all(outgoing, DP, 0, 0, tiled=True)
     second = swap_core(first)
-    partial, new_part = partial_values(where, kept, first, second, arrived, slot_order)
+    partial, new_part = partial_values(kept, first, second, arrived, slot_order)
     other = swap_section(partial)
     rows_turned = turned(kept, first, second)
     v_new_rows = (new_part + other[2 * row_count :])[:new_count]
-    product = weight_product(where, rows_turned, partial, other)
+    product = weight_product(rows_turned, partial, other)
     terms = lax.all_to_all(
         product.reshape(replicas, w_rows, width_local), DP, 0, 0, tiled=True
     )

time: 136 us -> 129 us (0.949)
  Pallas kernels: 17.5 us -> 12.3 us
  local copies, waits for them, and re-layouts: 6.25 us -> 2.79 us
    pallas_call x4, Pallas kernels: 17.5 us -> 12.3 us  [the longest x1 5.12 us: split_halves(): pl.pallas_call(halves_body, grid=(steps,), in_specs=[pl.BlockSpec((row_co...]
    all_to_all x1, waiting for transfers between devices: 25.5 us -> 23.6 us  [per_device(): lax.all_to_all(product.reshape(replicas, w_rows, width_local), DP, 0, 0,...]
    reshape x2 -> x1, local copies, waits for them, and re-layouts: 1.77 us -> 0.09 us  [partial_values(): slot_order.reshape(1, -1)]
    unnamed x19 -> x21, local copies, waits for them, and re-layouts: 2.22 us -> 0.56 us
  transfers between devices with their start and end apart: 5 -> 5, of which waited for: 3 -> 4; matrix products, arithmetic and copies ran while one was open for 6% -> 7% of each run, Pallas kernels for 3% -> 1%
where the time goes in v4:
time: 129 us; the launch traced here: 128 us
  starting transfers between devices  64.6 us (50%)
  waiting for transfers between devices  40.1 us (31%)
  Pallas kernels  12.3 us (10%)
  matrix products  4.57 us (4%)
  local copies, waits for them, and re-layouts  2.79 us (2%)
  other arithmetic  2.55 us (2%)
    ppermute x2, starting transfers between devices, swap_section(): return lax.ppermute(x, 'section', [(0, 1), (1, 0)])  31.6 us
    all_to_all x1, waiting for transfers between devices, per_device(): lax.all_to_all(product.reshape(replicas, w_rows, width_local), DP, 0, 0,...  23.6 us
    all_to_all x1, starting transfers between devices, per_device(): arrived = lax.all_to_all(outgoing, DP, 0, 0, tiled=True)  18.2 us
    ppermute x2, waiting for transfers between devices, swap_section(): return lax.ppermute(x, 'section', [(0, 1), (1, 0)])  15.8 us
    all_to_all x1, starting transfers between devices, per_device(): lax.all_to_all(product.reshape(replicas, w_rows, width_local), DP, 0, 0,...  12.8 us
    pallas_call x1, Pallas kernels, split_halves(): pl.pallas_call(halves_body, grid=(steps,), in_specs=[pl.BlockSpec((row_co...  5.12 us
    pallas_call x1, Pallas kernels, partial_values(): pl.pallas_call(partial_body, in_specs=[VMEM] * 5, out_specs=[VMEM, VMEM],...  2.92 us
    pallas_call x1, Pallas kernels, weight_product(): pl.pallas_call(product_body, in_specs=[VMEM] * 3, out_specs=VMEM, out_sha...  2.58 us
  transfers between devices with their start and end apart: 5, of which 4 were waited for; matrix products, arithmetic and copies ran while one was open for 7% of the time, Pallas kernels for 1%

profile of v4, /device:TPU:4, one launch (start us, length us, event | category | flops | bytes accessed | tf_op | source)
XLA Modules:
  0.0 127.7 jit_solution(5868340946995759630)
XLA Ops:
  0.6 0.0 copy-start
  0.6 5.1 %halves.1 = (bf16[144,4096]{1,0:T(8,128)(2,1)}, bf16[80,4096]{1,0:T(8,128)(2,1)}, bf16[64,72,128]{2,1,0:T(8,128)(2,1)}) custom-call(bf16[128,8192]{1,0:T(8,128)(2,1)} %rows_ref.1, bf16[3,4,8192]{2,1,0:T(4,128)(2,1)} %new_ref.1, bf16[64,128]{1,0:T(8,128)(2,1)} %w_ref.1, bf16[128,128]{1,0:T(8,128)(2,1)} %target_ref.1), custom_call_target="tpu_custom_call" | custom-call | flops 469762048 | bytes 4718592 | tf_op jit(solution)/shard_map/halves/pallas_call | solution.py:80
  5.8 0.0 copy-start.9
  5.8 0.0 copy-start.1
  5.8 18.2 %all-to-all-start = ((bf16[64,72,128]{2,1,0:T(8,128)(2,1)}), bf16[64,72,128]{2,1,0:T(8,128)(2,1)}, u32[]{:S(2)}, u32[]{:S(2)}) async-start(bf16[64,72,128]{2,1,0:T(8,128)(2,1)} %get-tuple-element.9), calls=%async_computation | async-start | bytes 2359296 | tf_op jit(solution)/shard_map/all_to_all | solution.py:261
  24.0 10.2 %collective-permute-start = (bf16[80,4096]{1,0:T(8,128)(2,1)}, bf16[80,4096]{1,0:T(8,128)(2,1)S(1)}, u32[]{:S(2)}, u32[]{:S(2)}) collective-permute-start(bf16[80,4096]{1,0:T(8,128)(2,1)} %get-tuple-element.8), channel_id=1, source_target_pairs={{0,1},{1,0},{2,3},{3,2},{4,5},{5,4},{6,7},{7,6},{8,9},{9,8},{10,11... | collective-permute-start | bytes 1966088 | tf_op jit(solution)/shard_map/ppermute | solution.py:228
  34.2 14.5 %collective-permute-done.first_ref = bf16[80,4096]{1,0:T(8,128)(2,1)S(1)} collective-permute-done((bf16[80,4096]{1,0:T(8,128)(2,1)}, bf16[80,4096]{1,0:T(8,128)(2,1)S(1)}, u32[]{:S(2)}, u32[]{:S(2)}) %collective-permute-start) | collective-permute-done | bytes 655392 | tf_op jit(solution)/shard_map/ppermute | solution.py:228
  48.7 1.9 %collective-permute-start.1 = (bf16[80,4096]{1,0:T(8,128)(2,1)S(1)}, bf16[80,4096]{1,0:T(8,128)(2,1)}, u32[]{:S(2)}, u32[]{:S(2)}) collective-permute-start(bf16[80,4096]{1,0:T(8,128)(2,1)S(1)} %collective-permute-done.first_ref), channel_id=1, source_target_pairs={{0,2},{2,0},{4,6},{6,4},{8,10},{10,8},{12,14},{14,12},{1,3},{3,1},... | collective-permute-start | bytes 1966088 | tf_op jit(solution)/shard_map/ppermute | solution.py:232
  50.7 0.5 broadcast.40
  51.2 0.0 copy-done.9
  51.2 0.7 reduce.11
  51.8 0.1 reshape_squeeze.3
  52.0 0.1 reshape.125.slot_ref
  52.1 0.8 collective-permute-done.1.second_ref
  52.8 0.0 all-to-all-done.block_ref
  52.9 0.0 copy-done.1
  52.9 2.9 %partial.1 = (f32[272,128]{1,0:T(8,128)}, f32[16,128]{1,0:T(8,128)S(1)}) custom-call(bf16[144,4096]{1,0:T(8,128)(2,1)S(1)} %copy-done.1, bf16[80,4096]{1,0:T(8,128)(2,1)S(1)} %collective-permute-done.first_ref, bf16[80,4096]{1,0:T(8,128)(2,1)} %collective-permute-done.1.second_ref, bf16[64,72,128]{2,1,0:T(8,128)(2,1)} %all-to-all-done.block_ref, ...), custom_call_target="tpu_custom_call" | custom-call | flops 318767104 | bytes 3538944 | tf_op jit(solution)/shard_map/partial/pallas_call | solution.py:146
  55.8 21.4 %collective-permute-start.2 = (f32[272,128]{1,0:T(8,128)}, f32[272,128]{1,0:T(8,128)S(1)}, u32[]{:S(2)}, u32[]{:S(2)}) collective-permute-start(f32[272,128]{1,0:T(8,128)} %get-tuple-element.11.mine_ref), channel_id=1, source_target_pairs={{0,1},{1,0},{2,3},{3,2},{4,5},{5,4},{6,7},{7,6},{8,9},{9,8},{10,11... | collective-permute-start | bytes 417800 | tf_op jit(solution)/shard_map/ppermute | solution.py:228
  77.2 1.4 %reshape.124 = bf16[3,4,8,128]{3,2,1,0:T(8,128)(2,1)} reshape(bf16[3,4,1024]{2,1,0:T(4,128)(2,1)} %param.12) | data formatting | bytes 49152 | tf_op jit(solution)/shard_map/reshape.2
  78.6 1.7 %turned.1.rows_ref = bf16[4096,256]{1,0:T(8,128)(2,1)S(1)} custom-call(bf16[144,4096]{1,0:T(8,128)(2,1)S(1)} %copy-done.1, bf16[80,4096]{1,0:T(8,128)(2,1)S(1)} %collective-permute-done.first_ref, bf16[80,4096]{1,0:T(8,128)(2,1)} %collective-permute-done.1.second_ref), custom_call_target="tpu_custom_call" | custom-call | bytes 4194304 | tf_op jit(solution)/shard_map/turned/pallas_call | solution.py:179
  80.3 1.2 collective-permute-done.2.other_ref
  81.5 2.6 %product.1 = bf16[4096,128]{1,0:T(8,128)(2,1)} custom-call(bf16[4096,256]{1,0:T(8,128)(2,1)S(1)} %turned.1.rows_ref, f32[272,128]{1,0:T(8,128)} %get-tuple-element.11.mine_ref, f32[272,128]{1,0:T(8,128)S(1)} %collective-permute-done.2.other_ref), custom_call_target="tpu_custom_call" | custom-call | flops 268435456 | bytes 3145728 | tf_op jit(solution)/shard_map/product/pallas_call | solution.py:212
  84.1 0.0 copy-start.2
  84.1 0.0 copy-start.8
  84.1 0.0 copy-start.7
  84.1 12.8 %all-to-all-start.1 = ((bf16[64,64,128]{2,1,0:T(8,128)(2,1)}), bf16[64,64,128]{2,1,0:T(8,128)(2,1)S(1)}, u32[]{:S(2)}, u32[]{:S(2)}) async-start(bf16[64,64,128]{2,1,0:T(8,128)(2,1)} %bitcast.10), calls=%async_computation.1 | async-start | bytes 2097152 | tf_op jit(solution)/shard_map/all_to_all | solution.py:268
  96.9 0.0 copy-done.2
  96.9 0.0 copy-done.8
  96.9 0.0 copy-start.6
  97.0 0.2 fusion.34
  97.2 0.0 copy-done.7
  97.2 0.0 copy-start.5
  97.2 0.1 iota_compare_fusion
  97.3 0.0 copy-done
  97.3 0.0 copy-start.3
  97.3 1.4 %fusion.33 = (f32[3,4,8]{2,1,0:T(4,128)S(1)}, f32[3,4,8,2048]{3,2,1,0:T(8,128)S(1)}) fusion(bf16[3,4,8,128]{3,2,1,0:T(8,128)(2,1)} %reshape.124, bf16[3,2048,128]{2,1,0:T(8,128)(2,1)S(1)} %copy-done, pred[3,2048]{1,0:T(4,128)(4,1)S(1)} %iota_compare_fusion), kind=kOutput, calls=%fused_computation.36 | convolution fusion | flops 50921376 | bytes 2390400 | tf_op jit(solution)/shard_map/ptgqd,pjgd->pgtqj/dot_general | solution.py:281
  98.8 0.0 copy-start.4
  98.8 0.1 fusion.22
  98.9 0.3 fusion.17
  99.2 0.0 copy-done.6
  99.2 0.0 copy-done.5
  99.2 0.6 add.18
  99.8 0.0 copy-done.3
  99.8 0.0 copy-done.4
  99.8 1.0 fusion.23
  100.8 1.9 %fusion.13 = bf16[3,4,1,8,128]{4,3,1,0,2:T(8,128)(2,1)S(1)} fusion(f32[3,128,4,8]{1,3,2,0:T(8,128)S(1)} %fusion.23, bf16[3,2048,128]{2,1,0:T(8,128)(2,1)} %param.15, f32[3,4,8,2048]{3,2,1,0:T(8,128)S(1)} %get-tuple-element.13, f32[3,4,8]{2,1,0:T(4,128)} %add.18, f32[3,4,8]{2,1,0:T(4,128)} %copy-done.4, pred[3,2048]{1,0:T(4,128)(4,1)} %copy-done.3), kind=kOutput, calls=%fused_computation.9 | convolution fusion | flops 51142656 | bytes 2439936 | tf_op jit(solution)/shard_map/pgtqj,pjgd->ptgqd/dot_general | solution.py:298
  102.7 0.6 convert_element_type.29
  103.3 23.6 %all-to-all-done.1 = bf16[64,64,128]{2,1,0:T(8,128)(2,1)S(1)} async-done(((bf16[64,64,128]{2,1,0:T(8,128)(2,1)}), bf16[64,64,128]{2,1,0:T(8,128)(2,1)S(1)}, u32[]{:S(2)}, u32[]{:S(2)}) %all-to-all-start.1) | async-done | bytes 1048608 | tf_op jit(solution)/shard_map/all_to_all | solution.py:268
  126.9 0.2 convert_reduce_fusion
  127.1 0.6 broadcast_multiply_fusion
  (6 shorter events, 0.0 us)
Async XLA Ops:
  0.6 96.7 %copy-start = (bf16[3,2048,128]{2,1,0:T(8,128)(2,1)S(1)}, bf16[3,2048,128]{2,1,0:T(8,128)(2,1)}, u32[]{:S(2)}) copy-start(bf16[3,2048,128]{2,1,0:T(8,128)(2,1)} %param.14) | copy-start | bytes 4718596
  5.8 45.4 %copy-start.9 = (s32[1,128]{1,0:T(1,128)S(1)}, s32[1,128]{1,0:T(1,128)}, u32[]{:S(2)}) copy-start(s32[1,128]{1,0:T(1,128)} %param.18) | copy-start | bytes 1540
  5.8 47.1 %copy-start.1 = (bf16[144,4096]{1,0:T(8,128)(2,1)S(1)}, bf16[144,4096]{1,0:T(8,128)(2,1)}, u32[]{:S(2)}) copy-start(bf16[144,4096]{1,0:T(8,128)(2,1)} %get-tuple-element.7.kept_ref) | copy-start | bytes 3538948
  5.8 47.1 %all-to-all-start = ((bf16[64,72,128]{2,1,0:T(8,128)(2,1)}), bf16[64,72,128]{2,1,0:T(8,128)(2,1)}, u32[]{:S(2)}, u32[]{:S(2)}) async-start(bf16[64,72,128]{2,1,0:T(8,128)(2,1)} %get-tuple-element.9), calls=%async_computation | async-start | bytes 2359296 | tf_op jit(solution)/shard_map/all_to_all | solution.py:261
  24.0 24.7 %collective-permute-start = (bf16[80,4096]{1,0:T(8,128)(2,1)}, bf16[80,4096]{1,0:T(8,128)(2,1)S(1)}, u32[]{:S(2)}, u32[]{:S(2)}) collective-permute-start(bf16[80,4096]{1,0:T(8,128)(2,1)} %get-tuple-element.8), channel_id=1, source_target_pairs={{0,1},{1,0},{2,3},{3,2},{4,5},{5,4},{6,7},{7,6},{8,9},{9,8},{10,11... | collective-permute-start | bytes 1966088 | tf_op jit(solution)/shard_map/ppermute | solution.py:228
  48.7 4.1 %collective-permute-start.1 = (bf16[80,4096]{1,0:T(8,128)(2,1)S(1)}, bf16[80,4096]{1,0:T(8,128)(2,1)}, u32[]{:S(2)}, u32[]{:S(2)}) collective-permute-start(bf16[80,4096]{1,0:T(8,128)(2,1)S(1)} %collective-permute-done.first_ref), channel_id=1, source_target_pairs={{0,2},{2,0},{4,6},{6,4},{8,10},{10,8},{12,14},{14,12},{1,3},{3,1},... | collective-permute-start | bytes 1966088 | tf_op jit(solution)/shard_map/ppermute | solution.py:232
  55.8 25.7 %collective-permute-start.2 = (f32[272,128]{1,0:T(8,128)}, f32[272,128]{1,0:T(8,128)S(1)}, u32[]{:S(2)}, u32[]{:S(2)}) collective-permute-start(f32[272,128]{1,0:T(8,128)} %get-tuple-element.11.mine_ref), channel_id=1, source_target_pairs={{0,1},{1,0},{2,3},{3,2},{4,5},{5,4},{6,7},{7,6},{8,9},{9,8},{10,11... | collective-permute-start | bytes 417800 | tf_op jit(solution)/shard_map/ppermute | solution.py:228
  84.1 12.9 %copy-start.2 = (bf16[3,4,8,128]{3,2,1,0:T(8,128)(2,1)S(1)}, bf16[3,4,8,128]{3,2,1,0:T(8,128)(2,1)}, u32[]{:S(2)}) copy-start(bf16[3,4,8,128]{3,2,1,0:T(8,128)(2,1)} %reshape.124) | copy-start | bytes 73732
  84.1 12.9 %copy-start.8 = (bf16[3,4,128]{2,1,0:T(4,128)(2,1)S(1)}, bf16[3,4,128]{2,1,0:T(4,128)(2,1)}, u32[]{:S(2)}) copy-start(bf16[3,4,128]{2,1,0:T(4,128)(2,1)} %param.13) | copy-start | bytes 9220
  84.1 13.1 %copy-start.7 = (s32[3]{0:T(128)S(1)}, s32[3]{0:T(128)}, u32[]{:S(2)}) copy-start(s32[3]{0:T(128)} %param.16) | copy-start | bytes 40
  84.1 42.8 %all-to-all-start.1 = ((bf16[64,64,128]{2,1,0:T(8,128)(2,1)}), bf16[64,64,128]{2,1,0:T(8,128)(2,1)S(1)}, u32[]{:S(2)}, u32[]{:S(2)}) async-start(bf16[64,64,128]{2,1,0:T(8,128)(2,1)} %bitcast.10), calls=%async_computation.1 | async-start | bytes 2097152 | tf_op jit(solution)/shard_map/all_to_all | solution.py:268
  96.9 2.2 %copy-start.6 = (pred[4,4]{1,0:T(4,128)(4,1)}, pred[4,4]{1,0:T(4,128)(4,1)S(1)}, u32[]{:S(2)}) copy-start(pred[4,4]{1,0:T(4,128)(4,1)S(1)} %iota_compare_fusion.1) | copy-start | bytes 52
  97.2 2.0 %copy-start.5 = (f32[3,4,8,4]{2,3,1,0:T(4,128)}, f32[3,4,8,4]{2,3,1,0:T(4,128)S(1)}, u32[]{:S(2)}) copy-start(f32[3,4,8,4]{2,3,1,0:T(4,128)S(1)} %get-tuple-element.15) | copy-start | bytes 4612
  97.3 2.5 %copy-start.3 = (pred[3,2048]{1,0:T(4,128)(4,1)}, pred[3,2048]{1,0:T(4,128)(4,1)S(1)}, u32[]{:S(2)}) copy-start(pred[3,2048]{1,0:T(4,128)(4,1)S(1)} %iota_compare_fusion) | copy-start | bytes 18436
  98.8 1.0 copy-start.4

commit v5 on v4

--- a/solution.py
+++ b/solution.py
@@ -33,31 +33,32 @@
     return lax.axis_index("tensor") % 2
 
 
-def halves_body(rows_ref, new_ref, w_ref, target_ref, keep_ref, send_ref, out_ref, new_scr):
-    section, core = lax.axis_index("section"), core_index()
-    row_count = rows_ref.shape[0]
-    half = row_count // 2
-    w_rows = w_ref.shape[0]
-    sent_at = pl.ds(pl.multiple_of(core * half, half), half)
-    own = picker(section, w_rows)
-    other = picker(1 - section, w_rows)
-
+def pick(block, which):
+    return jnp.dot(block, which, preferred_element_type=F32).astype(BF16)
+
+
+def fresh_rows(new_ref, new_scr):
     prompts, new, _ = new_ref.shape
     new_scr[...] = jnp.zeros_like(new_scr)
     for prompt in range(prompts):
         new_scr[prompt * new : (prompt + 1) * new, :] = new_ref[prompt].astype(F32)
 
-    def pick(block, which):
-        return jnp.dot(block, which, preferred_element_type=F32).astype(BF16)
-
-    for tile in range(rows_ref.shape[1] // (2 * LANES)):
+
+def tiles(width):
+    for tile in range(width // (2 * LANES)):
         wide = slice(tile * 2 * LANES, (tile + 1) * 2 * LANES)
         thin = slice(tile * LANES, (tile + 1) * LANES)
-        keep_ref[:row_count, thin] = pick(rows_ref[:, wide], own)
-        fresh = new_scr[:, wide].astype(BF16)
-        keep_ref[row_count:, thin] = pick(fresh, own)
-        send_ref[:half, thin] = pick(rows_ref[sent_at, wide], other)
-        send_ref[half:, thin] = pick(fresh, other)
+        yield wide, thin
+
+
+def sent_body(rows_ref, new_ref, w_ref, target_ref, send_ref, out_ref, new_scr):
+    half = rows_ref.shape[0]
+    w_rows = w_ref.shape[0]
+    other = picker(1 - lax.axis_index("section"), w_rows)
+    fresh_rows(new_ref, new_scr)
+    for wide, thin in tiles(rows_ref.shape[1]):
+        send_ref[:half, thin] = pick(rows_ref[:, wide], other)
+        send_ref[half:, thin] = pick(new_scr[:, wide].astype(BF16), other)
     peers = out_ref.shape[0]
     targets = target_ref.shape[0]
     per_peer = targets // peers
@@ -71,39 +72,72 @@
         out_ref[peer, w_rows:, :] = slots[peer]
 
 
-def split_halves(rows, new_rows, w_value, target, replicas):
+def sent_half(rows, new_rows, w_value, target, replicas):
     row_count, width = rows.shape
     w_rows, columns = w_value.shape
+    half = row_count // 2
     steps = 4
     block = width // steps
-    kept, sent = row_count + PAD, row_count // 2 + PAD
-    return pl.pallas_call(
-        halves_body,
+    sent = half + PAD
+    return pl.pallas_call(
+        sent_body,
+        grid=(steps,),
+        in_specs=[
+            pl.BlockSpec((half, block), lambda i: (core_index(), i)),
+            pl.BlockSpec((*new_rows.shape[:2], block), lambda i: (0, 0, i)),
+            pl.BlockSpec((w_rows, columns), lambda i: (0, 0)),
+            pl.BlockSpec((row_count // steps, columns), lambda i: (i, 0)),
+        ],
+        out_specs=[
+            pl.BlockSpec((sent, block // 2), lambda i: (0, i)),
+            pl.BlockSpec((replicas // steps, w_rows + SLOT, columns), lambda i: (i, 0, 0)),
+        ],
+        out_shape=[
+            jax.ShapeDtypeStruct((sent, width // 2), BF16),
+            jax.ShapeDtypeStruct((replicas, w_rows + SLOT, columns), BF16),
+        ],
+        cost_estimate=pl.CostEstimate(
+            flops=2 * sent * width * LANES,
+            bytes_accessed=4 * sent * width,
+            transcendentals=0,
+        ),
+        scratch_shapes=[pltpu.VMEM((PAD, block), F32)],
+        name="sent",
+    )(rows, new_rows, w_value, target)
+
+
+def kept_body(rows_ref, new_ref, keep_ref, new_scr, *, w_rows):
+    row_count = rows_ref.shape[0]
+    own = picker(lax.axis_index("section"), w_rows)
+    fresh_rows(new_ref, new_scr)
+    for wide, thin in tiles(rows_ref.shape[1]):
+        keep_ref[:row_count, thin] = pick(rows_ref[:, wide], own)
+        keep_ref[row_count:, thin] = pick(new_scr[:, wide].astype(BF16), own)
+
+
+def kept_half(rows, new_rows, w_rows):
+    row_count, width = rows.shape
+    steps = 4
+    block = width // steps
+    kept = row_count + PAD
+    return pl.pallas_call(
+        lambda *refs: kept_body(*refs, w_rows=w_rows),
         grid=(steps,),
         in_specs=[
             pl.BlockSpec((row_count, block), lambda i: (0, i)),
             pl.BlockSpec((*new_rows.shape[:2], block), lambda i: (0, 0, i)),
-            pl.BlockSpec((w_rows, columns), lambda i: (0, 0)),
-            pl.BlockSpec((row_count // steps, columns), lambda i: (i, 0)),
-        ],
-        out_specs=[
-            pl.BlockSpec((kept, block // 2), lambda i: (0, i)),
-            pl.BlockSpec((sent, block // 2), lambda i: (0, i)),
-            pl.BlockSpec((replicas // steps, w_rows + SLOT, columns), lambda i: (i, 0, 0)),
-        ],
-        out_shape=[
-            jax.ShapeDtypeStruct((kept, width // 2), BF16),
-            jax.ShapeDtypeStruct((sent, width // 2), BF16),
-            jax.ShapeDtypeStruct((replicas, w_rows + SLOT, columns), BF16),
-        ],
-        cost_estimate=pl.CostEstimate(
-            flops=2 * (kept + sent) * width * LANES,
-            bytes_accessed=4 * (row_count + PAD) * width,
+        ],
+        out_specs=pl.BlockSpec((kept, block // 2), lambda i: (0, i)),
+        out_shape=jax.ShapeDtypeStruct((kept, width // 2), BF16),
+        cost_estimate=pl.CostEstimate(
+            flops=2 * kept * width * LANES,
+            bytes_accessed=4 * kept * width,
             transcendentals=0,
         ),
         scratch_shapes=[pltpu.VMEM((PAD, block), F32)],
-        name="halves",
-    )(rows, new_rows, w_value, target)
+        compiler_params=pltpu.CompilerParams(vmem_limit_bytes=GRANT),
+        name="kept",
+    )(rows, new_rows)
 
 
 VMEM = pl.BlockSpec(memory_space=pltpu.VMEM)
@@ -254,9 +288,8 @@
         mb_map[0].reshape(replicas, per_peer), ((0, 0), (0, SLOT - per_peer)), constant_values=-1
     )
 
-    kept, sent, outgoing = split_halves(
-        sampled_rows, hidden_new, w_value, value_target, replicas
-    )
+    sent, outgoing = sent_half(sampled_rows, hidden_new, w_value, value_target, replicas)
+    kept = kept_half(sampled_rows, hidden_new, w_rows)
     first = swap_section(sent)
     arrived = lax.all_to_all(outgoing, DP, 0, 0, tiled=True)
     second = swap_core(first)
@@ -268,7 +301,7 @@
     terms = lax.all_to_all(
         product.reshape(replicas, w_rows, width_local), DP, 0, 0, tiled=True
     )
-    grad_value = jnp.sum(terms.astype(jnp.float32), axis=0) / row_count
+    grad_value = jnp.sum(terms.astype(jnp.float32) * (1.0 / row_count), axis=0)
     heads_local = width_local // HD
     cache_size = key_cache.shape[1]
     scale = 1.0 / jnp.sqrt(jnp.float32(HD))

time: 129 us -> 132 us (1.023)
  local copies, waits for them, and re-layouts: 2.79 us -> 5.3 us
    unnamed x21 -> x25, local copies, waits for them, and re-layouts: 0.56 us -> 3.07 us
    pallas_call x1 -> x2, Pallas kernels: 5.12 us -> 6.06 us  [the longest x1 4.36 us: sent_half(): pl.pallas_call(sent_body, grid=(steps,), in_specs=[pl.BlockSpec((half, bl...]
  transfers between devices with their start and end apart: 5 -> 5, of which waited for: 4 -> 3; matrix products, arithmetic and copies ran while one was open for 7% -> 7% of each run, Pallas kernels for 1% -> 3%
where the time goes in v5:
time: 132 us; the launch traced here: 131 us
  starting transfers between devices  64.6 us (49%)
  waiting for transfers between devices  40 us (30%)
  Pallas kernels  13.3 us (10%)
  local copies, waits for them, and re-layouts  5.3 us (4%)
  matrix products  4.57 us (3%)
  other arithmetic  2.61 us (2%)
    ppermute x2, starting transfers between devices, swap_section(): return lax.ppermute(x, 'section', [(0, 1), (1, 0)])  31.6 us
    all_to_all x1, waiting for transfers between devices, per_device(): lax.all_to_all(product.reshape(replicas, w_rows, width_local), DP, 0, 0,...  24 us
    all_to_all x1, starting transfers between devices, per_device(): arrived = lax.all_to_all(outgoing, DP, 0, 0, tiled=True)  18.2 us
    ppermute x2, waiting for transfers between devices, swap_section(): return lax.ppermute(x, 'section', [(0, 1), (1, 0)])  15.9 us
    all_to_all x1, starting transfers between devices, per_device(): lax.all_to_all(product.reshape(replicas, w_rows, width_local), DP, 0, 0,...  12.8 us
    pallas_call x1, Pallas kernels, sent_half(): pl.pallas_call(sent_body, grid=(steps,), in_specs=[pl.BlockSpec((half, bl...  4.36 us
    unnamed x25, local copies, waits for them, and re-layouts  3.07 us
    pallas_call x1, Pallas kernels, partial_values(): pl.pallas_call(partial_body, in_specs=[VMEM] * 5, out_specs=[VMEM, VMEM],...  2.94 us
  transfers between devices with their start and end apart: 5, of which 3 were waited for; matrix products, arithmetic and copies ran while one was open for 7% of the time, Pallas kernels for 3%

profile of v5, /device:TPU:4, one launch (start us, length us, event | category | flops | bytes accessed | tf_op | source)
XLA Modules:
  0.0 131.1 jit_solution(15016406959525819802)
XLA Ops:
  0.6 0.0 copy-start
  0.6 4.4 %sent.1 = (bf16[80,4096]{1,0:T(8,128)(2,1)}, bf16[64,72,128]{2,1,0:T(8,128)(2,1)}) custom-call(bf16[128,8192]{1,0:T(8,128)(2,1)} %rows_ref.1, bf16[3,4,8192]{2,1,0:T(4,128)(2,1)} %new_ref.1, bf16[64,128]{1,0:T(8,128)(2,1)} %w_ref.1, bf16[128,128]{1,0:T(8,128)(2,1)} %target_ref.1), custom_call_target="tpu_custom_call" | custom-call | flops 167772160 | bytes 2621440 | tf_op jit(solution)/shard_map/sent/pallas_call | solution.py:82
  5.0 0.0 copy-start.9
  5.0 0.0 copy-start.11
  5.0 18.2 %all-to-all-start = ((bf16[64,72,128]{2,1,0:T(8,128)(2,1)}), bf16[64,72,128]{2,1,0:T(8,128)(2,1)}, u32[]{:S(2)}, u32[]{:S(2)}) async-start(bf16[64,72,128]{2,1,0:T(8,128)(2,1)} %get-tuple-element.7), calls=%async_computation | async-start | bytes 2359296 | tf_op jit(solution)/shard_map/all_to_all | solution.py:294
  23.2 0.0 copy-done.9
  23.3 10.2 %collective-permute-start = (bf16[80,4096]{1,0:T(8,128)(2,1)S(1)}, bf16[80,4096]{1,0:T(8,128)(2,1)S(1)}, u32[]{:S(2)}, u32[]{:S(2)}) collective-permute-start(bf16[80,4096]{1,0:T(8,128)(2,1)S(1)} %copy-done.9), channel_id=1, source_target_pairs={{0,1},{1,0},{2,3},{3,2},{4,5},{5,4},{6,7},{7,6},{8,9},{9,8},{10,11... | collective-permute-start | bytes 1966088 | tf_op jit(solution)/shard_map/ppermute | solution.py:262
  33.4 14.3 %collective-permute-done.first_ref = bf16[80,4096]{1,0:T(8,128)(2,1)S(1)} collective-permute-done((bf16[80,4096]{1,0:T(8,128)(2,1)S(1)}, bf16[80,4096]{1,0:T(8,128)(2,1)S(1)}, u32[]{:S(2)}, u32[]{:S(2)}) %collective-permute-start) | collective-permute-done | bytes 655392 | tf_op jit(solution)/shard_map/ppermute | solution.py:262
  47.8 1.9 %collective-permute-start.1 = (bf16[80,4096]{1,0:T(8,128)(2,1)S(1)}, bf16[80,4096]{1,0:T(8,128)(2,1)}, u32[]{:S(2)}, u32[]{:S(2)}) collective-permute-start(bf16[80,4096]{1,0:T(8,128)(2,1)S(1)} %collective-permute-done.first_ref), channel_id=1, source_target_pairs={{0,2},{2,0},{4,6},{6,4},{8,10},{10,8},{12,14},{14,12},{1,3},{3,1},... | collective-permute-start | bytes 1966088 | tf_op jit(solution)/shard_map/ppermute | solution.py:266
  49.7 0.5 broadcast.39
  50.2 0.0 copy-done.11
  50.2 0.7 reduce.11
  50.9 0.1 reshape_squeeze.3
  51.0 0.1 reshape.125.slot_ref
  51.1 0.0 copy-start.1
  51.1 1.6 %copy-done.1 = bf16[128,8192]{1,0:T(8,128)(2,1)S(1)} copy-done((bf16[128,8192]{1,0:T(8,128)(2,1)S(1)}, bf16[128,8192]{1,0:T(8,128)(2,1)}, u32[]{:S(2)}) %copy-start.1) | copy-done | bytes 2097176
  52.7 0.0 copy-start.2
  52.7 0.9 copy-done.2
  53.6 1.7 %kept.1.kept_ref = bf16[144,4096]{1,0:T(8,128)(2,1)S(1)} custom-call(bf16[128,8192]{1,0:T(8,128)(2,1)S(1)} %copy-done.1, bf16[3,4,8192]{2,1,0:T(4,128)(2,1)S(1)} %copy-done.2), custom_call_target="tpu_custom_call" | custom-call | flops 301989888 | bytes 4718592 | tf_op jit(solution)/shard_map/kept/pallas_call | solution.py:123
  55.3 0.0 collective-permute-done.1.second_ref
  55.4 0.0 all-to-all-done.block_ref
  55.4 2.9 %partial.1 = (f32[272,128]{1,0:T(8,128)}, f32[16,128]{1,0:T(8,128)S(1)}) custom-call(bf16[144,4096]{1,0:T(8,128)(2,1)S(1)} %kept.1.kept_ref, bf16[80,4096]{1,0:T(8,128)(2,1)S(1)} %collective-permute-done.first_ref, bf16[80,4096]{1,0:T(8,128)(2,1)} %collective-permute-done.1.second_ref, bf16[64,72,128]{2,1,0:T(8,128)(2,1)} %all-to-all-done.block_ref, ...), custom_call_target="tpu_custom_call" | custom-call | flops 318767104 | bytes 3538944 | tf_op jit(solution)/shard_map/partial/pallas_call | solution.py:180
  58.3 21.4 %collective-permute-start.2 = (f32[272,128]{1,0:T(8,128)}, f32[272,128]{1,0:T(8,128)S(1)}, u32[]{:S(2)}, u32[]{:S(2)}) collective-permute-start(f32[272,128]{1,0:T(8,128)} %get-tuple-element.9.mine_ref), channel_id=1, source_target_pairs={{0,1},{1,0},{2,3},{3,2},{4,5},{5,4},{6,7},{7,6},{8,9},{9,8},{10,11... | collective-permute-start | bytes 417800 | tf_op jit(solution)/shard_map/ppermute | solution.py:262
  79.7 1.4 %reshape.124 = bf16[3,4,8,128]{3,2,1,0:T(8,128)(2,1)} reshape(bf16[3,4,1024]{2,1,0:T(4,128)(2,1)} %param.12) | data formatting | bytes 49152 | tf_op jit(solution)/shard_map/reshape.2
  81.1 1.7 %turned.1.rows_ref = bf16[4096,256]{1,0:T(8,128)(2,1)S(1)} custom-call(bf16[144,4096]{1,0:T(8,128)(2,1)S(1)} %kept.1.kept_ref, bf16[80,4096]{1,0:T(8,128)(2,1)S(1)} %collective-permute-done.first_ref, bf16[80,4096]{1,0:T(8,128)(2,1)} %collective-permute-done.1.second_ref), custom_call_target="tpu_custom_call" | custom-call | bytes 4194304 | tf_op jit(solution)/shard_map/turned/pallas_call | solution.py:213
  82.8 1.6 %collective-permute-done.2.other_ref = f32[272,128]{1,0:T(8,128)S(1)} collective-permute-done((f32[272,128]{1,0:T(8,128)}, f32[272,128]{1,0:T(8,128)S(1)}, u32[]{:S(2)}, u32[]{:S(2)}) %collective-permute-start.2) | collective-permute-done | bytes 139296 | tf_op jit(solution)/shard_map/ppermute | solution.py:262
  84.4 2.6 %product.1 = bf16[4096,128]{1,0:T(8,128)(2,1)} custom-call(bf16[4096,256]{1,0:T(8,128)(2,1)S(1)} %turned.1.rows_ref, f32[272,128]{1,0:T(8,128)} %get-tuple-element.9.mine_ref, f32[272,128]{1,0:T(8,128)S(1)} %collective-permute-done.2.other_ref), custom_call_target="tpu_custom_call" | custom-call | flops 268435456 | bytes 3145728 | tf_op jit(solution)/shard_map/product/pallas_call | solution.py:246
  87.0 0.0 copy-start.3
  87.0 0.0 copy-start.10
  87.0 0.0 copy-start.8
  87.0 12.8 %all-to-all-start.1 = ((bf16[64,64,128]{2,1,0:T(8,128)(2,1)}), bf16[64,64,128]{2,1,0:T(8,128)(2,1)S(1)}, u32[]{:S(2)}, u32[]{:S(2)}) async-start(bf16[64,64,128]{2,1,0:T(8,128)(2,1)} %bitcast.10), calls=%async_computation.1 | async-start | bytes 2097152 | tf_op jit(solution)/shard_map/all_to_all | solution.py:301
  99.8 0.0 copy-done.3
  99.8 0.0 copy-done.10
  99.8 0.0 copy-start.7
  99.8 0.2 fusion.34
  100.1 0.0 copy-done.8
  100.1 0.0 copy-start.6
  100.1 0.1 iota_compare_fusion
  100.2 0.0 copy-done
  100.2 0.0 copy-start.4
  100.2 1.4 %fusion.33 = (f32[3,4,8]{2,1,0:T(4,128)S(1)}, f32[3,4,8,2048]{3,2,1,0:T(8,128)S(1)}) fusion(bf16[3,4,8,128]{3,2,1,0:T(8,128)(2,1)} %reshape.124, bf16[3,2048,128]{2,1,0:T(8,128)(2,1)S(1)} %copy-done, pred[3,2048]{1,0:T(4,128)(4,1)S(1)} %iota_compare_fusion), kind=kOutput, calls=%fused_computation.35 | convolution fusion | flops 50921376 | bytes 2390400 | tf_op jit(solution)/shard_map/ptgqd,pjgd->pgtqj/dot_general | solution.py:314
  101.7 0.0 copy-start.5
  101.7 0.1 fusion.22
  101.8 0.3 fusion.17
  102.1 0.0 copy-done.7
  102.1 0.0 copy-done.6
  102.1 0.6 add.18
  102.7 0.0 copy-done.4
  102.7 0.0 copy-done.5
  102.7 1.0 fusion.23
  103.7 1.9 %fusion.13 = bf16[3,4,1,8,128]{4,3,1,0,2:T(8,128)(2,1)S(1)} fusion(f32[3,128,4,8]{1,3,2,0:T(8,128)S(1)} %fusion.23, bf16[3,2048,128]{2,1,0:T(8,128)(2,1)} %param.15, f32[3,4,8,2048]{3,2,1,0:T(8,128)S(1)} %get-tuple-element.11, f32[3,4,8]{2,1,0:T(4,128)} %add.18, f32[3,4,8]{2,1,0:T(4,128)} %copy-done.5, pred[3,2048]{1,0:T(4,128)(4,1)} %copy-done.4), kind=kOutput, calls=%fused_computation.9 | convolution fusion | flops 51142656 | bytes 2439936 | tf_op jit(solution)/shard_map/pgtqj,pjgd->ptgqd/dot_general | solution.py:331
  105.6 0.6 convert_element_type.29
  106.2 24.0 %all-to-all-done.1 = bf16[64,64,128]{2,1,0:T(8,128)(2,1)S(1)} async-done(((bf16[64,64,128]{2,1,0:T(8,128)(2,1)}), bf16[64,64,128]{2,1,0:T(8,128)(2,1)S(1)}, u32[]{:S(2)}, u32[]{:S(2)}) %all-to-all-start.1) | async-done | bytes 1048608 | tf_op jit(solution)/shard_map/all_to_all | solution.py:301
  130.3 0.8 multiply_reduce_fusion
  (6 shorter events, 0.0 us)
Async XLA Ops:
  0.6 99.6 %copy-start = (bf16[3,2048,128]{2,1,0:T(8,128)(2,1)S(1)}, bf16[3,2048,128]{2,1,0:T(8,128)(2,1)}, u32[]{:S(2)}) copy-start(bf16[3,2048,128]{2,1,0:T(8,128)(2,1)} %param.14) | copy-start | bytes 4718596
  5.0 18.2 %copy-start.9 = (bf16[80,4096]{1,0:T(8,128)(2,1)S(1)}, bf16[80,4096]{1,0:T(8,128)(2,1)}, u32[]{:S(2)}) copy-start(bf16[80,4096]{1,0:T(8,128)(2,1)} %get-tuple-element.6) | copy-start | bytes 1966084
  5.0 45.2 %copy-start.11 = (s32[1,128]{1,0:T(1,128)S(1)}, s32[1,128]{1,0:T(1,128)}, u32[]{:S(2)}) copy-start(s32[1,128]{1,0:T(1,128)} %param.18) | copy-start | bytes 1540
  5.0 50.3 %all-to-all-start = ((bf16[64,72,128]{2,1,0:T(8,128)(2,1)}), bf16[64,72,128]{2,1,0:T(8,128)(2,1)}, u32[]{:S(2)}, u32[]{:S(2)}) async-start(bf16[64,72,128]{2,1,0:T(8,128)(2,1)} %get-tuple-element.7), calls=%async_computation | async-start | bytes 2359296 | tf_op jit(solution)/shard_map/all_to_all | solution.py:294
  23.3 24.5 %collective-permute-start = (bf16[80,4096]{1,0:T(8,128)(2,1)S(1)}, bf16[80,4096]{1,0:T(8,128)(2,1)S(1)}, u32[]{:S(2)}, u32[]{:S(2)}) collective-permute-start(bf16[80,4096]{1,0:T(8,128)(2,1)S(1)} %copy-done.9), channel_id=1, source_target_pairs={{0,1},{1,0},{2,3},{3,2},{4,5},{5,4},{6,7},{7,6},{8,9},{9,8},{10,11... | collective-permute-start | bytes 1966088 | tf_op jit(solution)/shard_map/ppermute | solution.py:262
  47.8 7.6 %collective-permute-start.1 = (bf16[80,4096]{1,0:T(8,128)(2,1)S(1)}, bf16[80,4096]{1,0:T(8,128)(2,1)}, u32[]{:S(2)}, u32[]{:S(2)}) collective-permute-start(bf16[80,4096]{1,0:T(8,128)(2,1)S(1)} %collective-permute-done.first_ref), channel_id=1, source_target_pairs={{0,2},{2,0},{4,6},{6,4},{8,10},{10,8},{12,14},{14,12},{1,3},{3,1},... | collective-permute-start | bytes 1966088 | tf_op jit(solution)/shard_map/ppermute | solution.py:266
  51.1 1.6 %copy-start.1 = (bf16[128,8192]{1,0:T(8,128)(2,1)S(1)}, bf16[128,8192]{1,0:T(8,128)(2,1)}, u32[]{:S(2)}) copy-start(bf16[128,8192]{1,0:T(8,128)(2,1)} %rows_ref.1) | copy-start | bytes 6291460
  52.7 0.9 copy-start.2
  58.3 26.1 %collective-permute-start.2 = (f32[272,128]{1,0:T(8,128)}, f32[272,128]{1,0:T(8,128)S(1)}, u32[]{:S(2)}, u32[]{:S(2)}) collective-permute-start(f32[272,128]{1,0:T(8,128)} %get-tuple-element.9.mine_ref), channel_id=1, source_target_pairs={{0,1},{1,0},{2,3},{3,2},{4,5},{5,4},{6,7},{7,6},{8,9},{9,8},{10,11... | collective-permute-start | bytes 417800 | tf_op jit(solution)/shard_map/ppermute | solution.py:262
  87.0 12.9 %copy-start.3 = (bf16[3,4,8,128]{3,2,1,0:T(8,128)(2,1)S(1)}, bf16[3,4,8,128]{3,2,1,0:T(8,128)(2,1)}, u32[]{:S(2)}) copy-start(bf16[3,4,8,128]{3,2,1,0:T(8,128)(2,1)} %reshape.124) | copy-start | bytes 73732
  87.0 12.9 %copy-start.10 = (bf16[3,4,128]{2,1,0:T(4,128)(2,1)S(1)}, bf16[3,4,128]{2,1,0:T(4,128)(2,1)}, u32[]{:S(2)}) copy-start(bf16[3,4,128]{2,1,0:T(4,128)(2,1)} %param.13) | copy-start | bytes 9220
  87.0 13.1 %copy-start.8 = (s32[3]{0:T(128)S(1)}, s32[3]{0:T(128)}, u32[]{:S(2)}) copy-start(s32[3]{0:T(128)} %param.16) | copy-start | bytes 40
  87.0 43.3 %all-to-all-start.1 = ((bf16[64,64,128]{2,1,0:T(8,128)(2,1)}), bf16[64,64,128]{2,1,0:T(8,128)(2,1)S(1)}, u32[]{:S(2)}, u32[]{:S(2)}) async-start(bf16[64,64,128]{2,1,0:T(8,128)(2,1)} %bitcast.10), calls=%async_computation.1 | async-start | bytes 2097152 | tf_op jit(solution)/shard_map/all_to_all | solution.py:301
  99.8 2.2 %copy-start.7 = (pred[4,4]{1,0:T(4,128)(4,1)}, pred[4,4]{1,0:T(4,128)(4,1)S(1)}, u32[]{:S(2)}) copy-start(pred[4,4]{1,0:T(4,128)(4,1)S(1)} %iota_compare_fusion.1) | copy-start | bytes 52
  100.1 2.0 %copy-start.6 = (f32[3,4,8,4]{2,3,1,0:T(4,128)}, f32[3,4,8,4]{2,3,1,0:T(4,128)S(1)}, u32[]{:S(2)}) copy-start(f32[3,4,8,4]{2,3,1,0:T(4,128)S(1)} %get-tuple-element.13) | copy-start | bytes 4612
  100.2 2.5 %copy-start.4 = (pred[3,2048]{1,0:T(4,128)(4,1)}, pred[3,2048]{1,0:T(4,128)(4,1)S(1)}, u32[]{:S(2)}) copy-start(pred[3,2048]{1,0:T(4,128)(4,1)S(1)} %iota_compare_fusion) | copy-start | bytes 18436
  101.7 1.0 copy-start.5

commit v6 on v5

--- a/solution.py
+++ b/solution.py
@@ -143,56 +143,69 @@
 VMEM = pl.BlockSpec(memory_space=pltpu.VMEM)
 
 
-def partial_body(
-    kept_ref, first_ref, second_ref, block_ref, slot_ref, out_ref, new_ref
-):
+def theirs_body(first_ref, second_ref, block_ref, out_ref):
     core = core_index()
     peers, block_rows, columns = block_ref.shape
     w_rows = block_rows - SLOT
-    kept, half = kept_ref.shape[0], first_ref.shape[0] - PAD
-    row_count = kept - PAD
+    half = first_ref.shape[0] - PAD
+    weights = block_ref[:, :w_rows, :].reshape(peers * w_rows, columns)
+    first_part = jnp.dot(first_ref[...], weights, preferred_element_type=F32)
+    second_part = jnp.dot(second_ref[:half, :], weights, preferred_element_type=F32)
+    near = pl.ds(pl.multiple_of(core * half, half), half)
+    far = pl.ds(pl.multiple_of((1 - core) * half, half), half)
+    out_ref[near, :] = first_part[:half]
+    out_ref[far, :] = second_part
+    out_ref[2 * half :, :] = first_part[half:]
+
+
+def theirs_values(first, second, arrived):
+    columns = arrived.shape[2]
+    rows, width = first.shape
+    return pl.pallas_call(
+        theirs_body,
+        in_specs=[VMEM] * 3,
+        out_specs=VMEM,
+        out_shape=jax.ShapeDtypeStruct((2 * rows - PAD, columns), F32),
+        cost_estimate=pl.CostEstimate(
+            flops=4 * width * columns * rows,
+            bytes_accessed=2 * width * (2 * rows + columns),
+            transcendentals=0,
+        ),
+        compiler_params=pltpu.CompilerParams(vmem_limit_bytes=GRANT),
+        name="theirs",
+    )(first, second, arrived)
+
+
+def mine_body(kept_ref, block_ref, slot_ref, out_ref):
+    peers, block_rows, columns = block_ref.shape
+    w_rows = block_rows - SLOT
+    row_count = kept_ref.shape[0] - PAD
     weights = block_ref[:, :w_rows, :].reshape(peers * w_rows, columns)
     slots = block_ref[:, w_rows:, :].reshape(peers * SLOT, columns)
     at = lax.broadcasted_iota(jnp.int32, (row_count, peers * SLOT), 0)
     place = one_hot(at == slot_ref[...])
     targets = jnp.dot(place, slots, preferred_element_type=F32)
-
-    def times(rows):
-        return jnp.dot(rows, weights, preferred_element_type=F32)
-
-    kept_part = times(kept_ref[...])
-    first_part = times(first_ref[...])
-    second_part = times(second_ref[:half, :])
-    near = pl.ds(pl.multiple_of(row_count + core * half, half), half)
-    far = pl.ds(pl.multiple_of(row_count + (1 - core) * half, half), half)
+    kept_part = jnp.dot(kept_ref[...], weights, preferred_element_type=F32)
     out_ref[:row_count, :] = kept_part[:row_count] - targets
-    out_ref[near, :] = first_part[:half]
-    out_ref[far, :] = second_part
-    out_ref[2 * row_count :, :] = first_part[half:]
-    new_ref[...] = kept_part[row_count:]
-
-
-def partial_values(kept, first, second, arrived, slot_order):
+    out_ref[row_count:, :] = kept_part[row_count:]
+
+
+def mine_values(kept, arrived, slot_order):
     columns = arrived.shape[2]
-    width = kept.shape[1]
-    row_count = kept.shape[0] - PAD
-    rows = kept.shape[0] + 2 * first.shape[0]
-    return pl.pallas_call(
-        partial_body,
-        in_specs=[VMEM] * 5,
-        out_specs=[VMEM, VMEM],
-        out_shape=[
-            jax.ShapeDtypeStruct((2 * row_count + PAD, columns), F32),
-            jax.ShapeDtypeStruct((PAD, columns), F32),
-        ],
+    rows, width = kept.shape
+    return pl.pallas_call(
+        mine_body,
+        in_specs=[VMEM] * 3,
+        out_specs=VMEM,
+        out_shape=jax.ShapeDtypeStruct((rows, columns), F32),
         cost_estimate=pl.CostEstimate(
             flops=2 * width * columns * rows,
             bytes_accessed=2 * width * (rows + columns),
             transcendentals=0,
         ),
         compiler_params=pltpu.CompilerParams(vmem_limit_bytes=GRANT),
-        name="partial",
-    )(kept, first, second, arrived, slot_order.reshape(1, -1))
+        name="mine",
+    )(kept, arrived, slot_order.reshape(1, -1))
 
 
 def turn_body(kept_ref, first_ref, second_ref, out_ref):
@@ -223,29 +236,27 @@
     )(kept, first, second)
 
 
-def product_body(rows_ref, mine_ref, other_ref, out_ref):
+def product_body(rows_ref, mine_ref, theirs_ref, its_mine_ref, its_theirs_ref, out_ref):
     core = core_index()
-    row_count = rows_ref.shape[1] // 2
+    row_count = mine_ref.shape[0] - PAD
     half = row_count // 2
-
-    def residual(at, its_at, size):
-        return (mine_ref[pl.ds(at, size), :] + other_ref[pl.ds(its_at, size), :]).astype(BF16)
-
-    near = pl.multiple_of(core * half, half)
-    far = pl.multiple_of((1 - core) * half, half)
-    own = residual(0, row_count, row_count)
-    first = residual(row_count + near, near, half)
-    second = residual(row_count + far, far, half)
-    residuals = jnp.concatenate([own, first, second], axis=0)
+    own = (mine_ref[:row_count, :] + its_theirs_ref[:row_count, :]).astype(BF16)
+
+    def residual(at):
+        at = pl.ds(pl.multiple_of(at, half), half)
+        return (theirs_ref[at, :] + its_mine_ref[at, :]).astype(BF16)
+
+    residuals = [own, residual(core * half), residual((1 - core) * half)]
+    residuals = jnp.concatenate(residuals, axis=0)
     out_ref[...] = jnp.dot(rows_ref[...], residuals, preferred_element_type=F32).astype(BF16)
 
 
-def weight_product(rows, mine, other):
+def weight_product(rows, mine, theirs, its_mine, its_theirs):
     width, both = rows.shape
     columns = mine.shape[1]
     return pl.pallas_call(
         product_body,
-        in_specs=[VMEM] * 3,
+        in_specs=[VMEM] * 5,
         out_specs=VMEM,
         out_shape=jax.ShapeDtypeStruct((width, columns), BF16),
         cost_estimate=pl.CostEstimate(
@@ -255,7 +266,7 @@
         ),
         compiler_params=pltpu.CompilerParams(vmem_limit_bytes=GRANT),
         name="product",
-    )(rows, mine, other)
+    )(rows, mine, theirs, its_mine, its_theirs)
 
 
 def swap_section(x):
@@ -293,11 +304,13 @@
     first = swap_section(sent)
     arrived = lax.all_to_all(outgoing, DP, 0, 0, tiled=True)
     second = swap_core(first)
-    partial, new_part = partial_values(kept, first, second, arrived, slot_order)
-    other = swap_section(partial)
+    theirs = theirs_values(first, second, arrived)
+    its_theirs = swap_section(theirs)
+    mine = mine_values(kept, arrived, slot_order)
+    its_mine = swap_section(mine)
     rows_turned = turned(kept, first, second)
-    v_new_rows = (new_part + other[2 * row_count :])[:new_count]
-    product = weight_product(rows_turned, partial, other)
+    v_new_rows = (mine[row_count:] + its_theirs[row_count:])[:new_count]
+    product = weight_product(rows_turned, mine, theirs, its_mine, its_theirs)
     terms = lax.all_to_all(
         product.reshape(replicas, w_rows, width_local), DP, 0, 0, tiled=True
     )

time: 132 us -> 139 us (1.053)
  waiting for transfers between devices: 40 us -> 44.8 us
  local copies, waits for them, and re-layouts: 5.3 us -> 7.25 us
  starting transfers between devices: 64.6 us -> 66.5 us
  matrix products: 4.57 us -> 3.05 us
    ppermute x2 -> x3, waiting for transfers between devices: 15.9 us -> 21.2 us  [swap_section(): return lax.ppermute(x, 'section', [(0, 1), (1, 0)])]
    ppermute x2 -> x3, starting transfers between devices: 31.6 us -> 33.5 us  [swap_section(): return lax.ppermute(x, 'section', [(0, 1), (1, 0)])]
    pallas_call x2 -> x3, Pallas kernels: 5.53 us -> 6.34 us  [the longest x1 2.61 us: weight_product(): pl.pallas_call(product_body, in_specs=[VMEM] * 5, out_specs=VMEM, out_sha...]
    unnamed x25 -> x19, local copies, waits for them, and re-layouts: 3.07 us -> 3.73 us
  transfers between devices with their start and end apart: 5 -> 6, of which waited for: 3 -> 3; matrix products, arithmetic and copies ran while one was open for 7% -> 6% of each run, Pallas kernels for 3% -> 4%
where the time goes in v6:
time: 139 us
  starting transfers between devices  66.5 us (48%)
  waiting for transfers between devices  44.8 us (32%)
  Pallas kernels  14 us (10%)
  local copies, waits for them, and re-layouts  7.25 us (5%)
  matrix products  3.05 us (2%)
  other arithmetic  2.02 us (1%)
    ppermute x3, starting transfers between devices, swap_section(): return lax.ppermute(x, 'section', [(0, 1), (1, 0)])  33.5 us
    all_to_all x1, waiting for transfers between devices, per_device(): lax.all_to_all(product.reshape(replicas, w_rows, width_local), DP, 0, 0,...  23.6 us
    ppermute x3, waiting for transfers between devices, swap_section(): return lax.ppermute(x, 'section', [(0, 1), (1, 0)])  21.2 us
    all_to_all x1, starting transfers between devices, per_device(): arrived = lax.all_to_all(outgoing, DP, 0, 0, tiled=True)  18.2 us
    all_to_all x1, starting transfers between devices, per_device(): lax.all_to_all(product.reshape(replicas, w_rows, width_local), DP, 0, 0,...  12.8 us
    pallas_call x1, Pallas kernels, sent_half(): pl.pallas_call(sent_body, grid=(steps,), in_specs=[pl.BlockSpec((half, bl...  4.31 us
    unnamed x19, local copies, waits for them, and re-layouts  3.73 us
  transfers between devices with their start and end apart: 6, of which 3 were waited for; matrix products, arithmetic and copies ran while one was open for 6% of the time, Pallas kernels for 4%

profile of v6, /device:TPU:4, one launch (start us, length us, event | category | flops | bytes accessed | tf_op | source)
XLA Modules:
  0.0 138.5 jit_solution(3280496670482795919)
XLA Ops:
  0.6 0.0 copy-start
  0.6 4.3 %sent.1 = (bf16[80,4096]{1,0:T(8,128)(2,1)}, bf16[64,72,128]{2,1,0:T(8,128)(2,1)}) custom-call(bf16[128,8192]{1,0:T(8,128)(2,1)} %rows_ref.1, bf16[3,4,8192]{2,1,0:T(4,128)(2,1)} %new_ref.1, bf16[64,128]{1,0:T(8,128)(2,1)} %w_ref.1, bf16[128,128]{1,0:T(8,128)(2,1)} %target_ref.1), custom_call_target="tpu_custom_call" | custom-call | flops 167772160 | bytes 2621440 | tf_op jit(solution)/shard_map/sent/pallas_call | solution.py:82
  5.0 0.0 copy-start.6
  5.0 0.0 copy-start.8
  5.0 18.2 %all-to-all-start = ((bf16[64,72,128]{2,1,0:T(8,128)(2,1)}), bf16[64,72,128]{2,1,0:T(8,128)(2,1)}, u32[]{:S(2)}, u32[]{:S(2)}) async-start(bf16[64,72,128]{2,1,0:T(8,128)(2,1)} %get-tuple-element.4), calls=%async_computation | async-start | bytes 2359296 | tf_op jit(solution)/shard_map/all_to_all | solution.py:305
  23.2 0.0 copy-done.6
  23.2 10.2 %collective-permute-start = (bf16[80,4096]{1,0:T(8,128)(2,1)S(1)}, bf16[80,4096]{1,0:T(8,128)(2,1)S(1)}, u32[]{:S(2)}, u32[]{:S(2)}) collective-permute-start(bf16[80,4096]{1,0:T(8,128)(2,1)S(1)} %copy-done.6), channel_id=1, source_target_pairs={{0,1},{1,0},{2,3},{3,2},{4,5},{5,4},{6,7},{7,6},{8,9},{9,8},{10,11... | collective-permute-start | bytes 1966088 | tf_op jit(solution)/shard_map/ppermute | solution.py:273
  33.4 14.3 %collective-permute-done.first_ref = bf16[80,4096]{1,0:T(8,128)(2,1)S(1)} collective-permute-done((bf16[80,4096]{1,0:T(8,128)(2,1)S(1)}, bf16[80,4096]{1,0:T(8,128)(2,1)S(1)}, u32[]{:S(2)}, u32[]{:S(2)}) %collective-permute-start) | collective-permute-done | bytes 655392 | tf_op jit(solution)/shard_map/ppermute | solution.py:273
  47.7 1.9 %collective-permute-start.1 = (bf16[80,4096]{1,0:T(8,128)(2,1)S(1)}, bf16[80,4096]{1,0:T(8,128)(2,1)}, u32[]{:S(2)}, u32[]{:S(2)}) collective-permute-start(bf16[80,4096]{1,0:T(8,128)(2,1)S(1)} %collective-permute-done.first_ref), channel_id=1, source_target_pairs={{0,2},{2,0},{4,6},{6,4},{8,10},{10,8},{12,14},{14,12},{1,3},{3,1},... | collective-permute-start | bytes 1966088 | tf_op jit(solution)/shard_map/ppermute | solution.py:277
  49.6 0.5 broadcast.39
  50.2 0.0 copy-done.8
  50.2 0.7 reduce.11
  50.8 0.1 reshape_squeeze.3
  51.0 0.7 reshape.125.slot_ref
  51.6 0.0 copy-start.1
  51.6 1.6 %copy-done.1 = bf16[128,8192]{1,0:T(8,128)(2,1)S(1)} copy-done((bf16[128,8192]{1,0:T(8,128)(2,1)S(1)}, bf16[128,8192]{1,0:T(8,128)(2,1)}, u32[]{:S(2)}) %copy-start.1) | copy-done | bytes 2097176
  53.2 0.0 copy-start.2
  53.2 0.9 copy-done.2
  54.2 1.7 %kept.1.kept_ref = bf16[144,4096]{1,0:T(8,128)(2,1)S(1)} custom-call(bf16[128,8192]{1,0:T(8,128)(2,1)S(1)} %copy-done.1, bf16[3,4,8192]{2,1,0:T(4,128)(2,1)S(1)} %copy-done.2), custom_call_target="tpu_custom_call" | custom-call | flops 301989888 | bytes 4718592 | tf_op jit(solution)/shard_map/kept/pallas_call | solution.py:123
  55.9 0.0 collective-permute-done.1.second_ref
  55.9 0.0 all-to-all-done.block_ref
  55.9 1.9 %theirs.1.theirs_ref = f32[144,128]{1,0:T(8,128)S(1)} custom-call(bf16[80,4096]{1,0:T(8,128)(2,1)S(1)} %collective-permute-done.first_ref, bf16[80,4096]{1,0:T(8,128)(2,1)} %collective-permute-done.1.second_ref, bf16[64,72,128]{2,1,0:T(8,128)(2,1)} %all-to-all-done.block_ref), custom_call_target="tpu_custom_call" | custom-call | flops 167772160 | bytes 2359296 | tf_op jit(solution)/shard_map/theirs/pallas_call | solution.py:164
  57.9 21.4 %collective-permute-start.2 = (f32[144,128]{1,0:T(8,128)S(1)}, f32[144,128]{1,0:T(8,128)}, u32[]{:S(2)}, u32[]{:S(2)}) collective-permute-start(f32[144,128]{1,0:T(8,128)S(1)} %theirs.1.theirs_ref), channel_id=1, source_target_pairs={{0,1},{1,0},{2,3},{3,2},{4,5},{5,4},{6,7},{7,6},{8,9},{9,8},{10,11... | collective-permute-start | bytes 221192 | tf_op jit(solution)/shard_map/ppermute | solution.py:273
  79.3 0.0 copy-start.3
  79.3 0.7 copy-done.3
  80.0 1.8 %mine.1.mine_ref = f32[144,128]{1,0:T(8,128)S(1)} custom-call(bf16[144,4096]{1,0:T(8,128)(2,1)S(1)} %kept.1.kept_ref, bf16[64,72,128]{2,1,0:T(8,128)(2,1)} %all-to-all-done.block_ref, s32[1,512]{1,0:T(1,128)S(1)} %copy-done.3), custom_call_target="tpu_custom_call" | custom-call | flops 150994944 | bytes 2228224 | tf_op jit(solution)/shard_map/mine/pallas_call | solution.py:196
  81.8 1.9 %collective-permute-start.3 = (f32[144,128]{1,0:T(8,128)S(1)}, f32[144,128]{1,0:T(8,128)}, u32[]{:S(2)}, u32[]{:S(2)}) collective-permute-start(f32[144,128]{1,0:T(8,128)S(1)} %mine.1.mine_ref), channel_id=1, source_target_pairs={{0,1},{1,0},{2,3},{3,2},{4,5},{5,4},{6,7},{7,6},{8,9},{9,8},{10,11... | collective-permute-start | bytes 221192 | tf_op jit(solution)/shard_map/ppermute | solution.py:273
  83.7 1.4 reshape.124
  85.1 1.7 %turned.1.rows_ref = bf16[4096,256]{1,0:T(8,128)(2,1)S(1)} custom-call(bf16[144,4096]{1,0:T(8,128)(2,1)S(1)} %kept.1.kept_ref, bf16[80,4096]{1,0:T(8,128)(2,1)S(1)} %collective-permute-done.first_ref, bf16[80,4096]{1,0:T(8,128)(2,1)} %collective-permute-done.1.second_ref), custom_call_target="tpu_custom_call" | custom-call | bytes 4194304 | tf_op jit(solution)/shard_map/turned/pallas_call | solution.py:226
  86.8 0.0 collective-permute-done.2.its_theirs_ref
  86.8 6.9 %collective-permute-done.3.its_mine_ref = f32[144,128]{1,0:T(8,128)} collective-permute-done((f32[144,128]{1,0:T(8,128)S(1)}, f32[144,128]{1,0:T(8,128)}, u32[]{:S(2)}, u32[]{:S(2)}) %collective-permute-start.3) | collective-permute-done | bytes 73760 | tf_op jit(solution)/shard_map/ppermute | solution.py:273
  93.6 2.6 %product.1 = bf16[4096,128]{1,0:T(8,128)(2,1)} custom-call(bf16[4096,256]{1,0:T(8,128)(2,1)S(1)} %turned.1.rows_ref, f32[144,128]{1,0:T(8,128)S(1)} %mine.1.mine_ref, f32[144,128]{1,0:T(8,128)S(1)} %theirs.1.theirs_ref, f32[144,128]{1,0:T(8,128)} %collective-permute-done.3.its_mine_ref, f32[144,128]{1,0:T(8,128)} %collective-permute-done.2.its_theirs_ref), custom_call_target="tpu_custom_call" | custom-call | flops 268435456 | bytes 3145728 | tf_op jit(solution)/shard_map/product/pallas_call | solution.py:257
  96.2 0.0 copy-start.4
  96.2 0.0 copy-start.7
  96.3 0.0 copy-start.5
  96.3 12.8 %all-to-all-start.1 = ((bf16[64,64,128]{2,1,0:T(8,128)(2,1)}), bf16[64,64,128]{2,1,0:T(8,128)(2,1)S(1)}, u32[]{:S(2)}, u32[]{:S(2)}) async-start(bf16[64,64,128]{2,1,0:T(8,128)(2,1)} %bitcast.10), calls=%async_computation.1 | async-start | bytes 2097152 | tf_op jit(solution)/shard_map/all_to_all | solution.py:314
  109.1 0.0 copy-done.4
  109.1 0.0 copy-done.7
  109.1 0.2 fusion.34
  109.4 0.0 copy-done.5
  109.4 0.1 iota_compare_fusion
  109.5 0.0 copy-done
  109.5 0.7 fusion.33
  110.2 0.1 fusion.22
  110.3 0.3 fusion.17
  110.6 0.7 slice.14
  111.3 0.3 fusion.23
  111.6 1.8 %fusion.13 = bf16[3,4,1,8,128]{4,3,1,0,2:T(8,128)(2,1)S(1)} fusion(f32[3,128,4,8]{1,3,2,0:T(8,128)S(1)} %fusion.23, bf16[3,2048,128]{2,1,0:T(8,128)(2,1)} %param.15, f32[3,4,8,2048]{3,2,1,0:T(8,128)S(1)} %get-tuple-element.7, f32[3,4,8]{2,1,0:T(4,128)S(1)} %add.18, f32[3,4,8]{2,1,0:T(4,128)S(1)} %max.9, pred[3,2048]{1,0:T(4,128)(4,1)S(1)} %iota_compare_fusion), kind=kOutput, calls=%fused_computation.9 | convolution fusion | flops 51142656 | bytes 2439936 | tf_op jit(solution)/shard_map/pgtqj,pjgd->ptgqd/dot_general | solution.py:344
  113.4 0.6 convert_element_type.29
  114.1 23.6 %all-to-all-done.1 = bf16[64,64,128]{2,1,0:T(8,128)(2,1)S(1)} async-done(((bf16[64,64,128]{2,1,0:T(8,128)(2,1)}), bf16[64,64,128]{2,1,0:T(8,128)(2,1)S(1)}, u32[]{:S(2)}, u32[]{:S(2)}) %all-to-all-start.1) | async-done | bytes 1048608 | tf_op jit(solution)/shard_map/all_to_all | solution.py:314
  137.7 0.9 multiply_reduce_fusion
  (7 shorter events, 0.1 us)
Async XLA Ops:
  0.6 108.8 %copy-start = (bf16[3,2048,128]{2,1,0:T(8,128)(2,1)S(1)}, bf16[3,2048,128]{2,1,0:T(8,128)(2,1)}, u32[]{:S(2)}) copy-start(bf16[3,2048,128]{2,1,0:T(8,128)(2,1)} %param.14) | copy-start | bytes 4718596
  5.0 18.2 %copy-start.6 = (bf16[80,4096]{1,0:T(8,128)(2,1)S(1)}, bf16[80,4096]{1,0:T(8,128)(2,1)}, u32[]{:S(2)}) copy-start(bf16[80,4096]{1,0:T(8,128)(2,1)} %get-tuple-element.5) | copy-start | bytes 1966084
  5.0 45.2 %copy-start.8 = (s32[1,128]{1,0:T(1,128)S(1)}, s32[1,128]{1,0:T(1,128)}, u32[]{:S(2)}) copy-start(s32[1,128]{1,0:T(1,128)} %param.18) | copy-start | bytes 1540
  5.0 50.9 %all-to-all-start = ((bf16[64,72,128]{2,1,0:T(8,128)(2,1)}), bf16[64,72,128]{2,1,0:T(8,128)(2,1)}, u32[]{:S(2)}, u32[]{:S(2)}) async-start(bf16[64,72,128]{2,1,0:T(8,128)(2,1)} %get-tuple-element.4), calls=%async_computation | async-start | bytes 2359296 | tf_op jit(solution)/shard_map/all_to_all | solution.py:305
  23.2 24.5 %collective-permute-start = (bf16[80,4096]{1,0:T(8,128)(2,1)S(1)}, bf16[80,4096]{1,0:T(8,128)(2,1)S(1)}, u32[]{:S(2)}, u32[]{:S(2)}) collective-permute-start(bf16[80,4096]{1,0:T(8,128)(2,1)S(1)} %copy-done.6), channel_id=1, source_target_pairs={{0,1},{1,0},{2,3},{3,2},{4,5},{5,4},{6,7},{7,6},{8,9},{9,8},{10,11... | collective-permute-start | bytes 1966088 | tf_op jit(solution)/shard_map/ppermute | solution.py:273
  47.7 8.2 %collective-permute-start.1 = (bf16[80,4096]{1,0:T(8,128)(2,1)S(1)}, bf16[80,4096]{1,0:T(8,128)(2,1)}, u32[]{:S(2)}, u32[]{:S(2)}) collective-permute-start(bf16[80,4096]{1,0:T(8,128)(2,1)S(1)} %collective-permute-done.first_ref), channel_id=1, source_target_pairs={{0,2},{2,0},{4,6},{6,4},{8,10},{10,8},{12,14},{14,12},{1,3},{3,1},... | collective-permute-start | bytes 1966088 | tf_op jit(solution)/shard_map/ppermute | solution.py:277
  51.6 1.6 %copy-start.1 = (bf16[128,8192]{1,0:T(8,128)(2,1)S(1)}, bf16[128,8192]{1,0:T(8,128)(2,1)}, u32[]{:S(2)}) copy-start(bf16[128,8192]{1,0:T(8,128)(2,1)} %rows_ref.1) | copy-start | bytes 6291460
  53.2 0.9 copy-start.2
  57.9 28.9 %collective-permute-start.2 = (f32[144,128]{1,0:T(8,128)S(1)}, f32[144,128]{1,0:T(8,128)}, u32[]{:S(2)}, u32[]{:S(2)}) collective-permute-start(f32[144,128]{1,0:T(8,128)S(1)} %theirs.1.theirs_ref), channel_id=1, source_target_pairs={{0,1},{1,0},{2,3},{3,2},{4,5},{5,4},{6,7},{7,6},{8,9},{9,8},{10,11... | collective-permute-start | bytes 221192 | tf_op jit(solution)/shard_map/ppermute | solution.py:273
  79.3 0.7 copy-start.3
  81.8 11.9 %collective-permute-start.3 = (f32[144,128]{1,0:T(8,128)S(1)}, f32[144,128]{1,0:T(8,128)}, u32[]{:S(2)}, u32[]{:S(2)}) collective-permute-start(f32[144,128]{1,0:T(8,128)S(1)} %mine.1.mine_ref), channel_id=1, source_target_pairs={{0,1},{1,0},{2,3},{3,2},{4,5},{5,4},{6,7},{7,6},{8,9},{9,8},{10,11... | collective-permute-start | bytes 221192 | tf_op jit(solution)/shard_map/ppermute | solution.py:273
  96.2 12.9 %copy-start.4 = (bf16[3,4,8,128]{3,2,1,0:T(8,128)(2,1)S(1)}, bf16[3,4,8,128]{3,2,1,0:T(8,128)(2,1)}, u32[]{:S(2)}) copy-start(bf16[3,4,8,128]{3,2,1,0:T(8,128)(2,1)} %reshape.124) | copy-start | bytes 73732
  96.2 12.9 %copy-start.7 = (bf16[3,4,128]{2,1,0:T(4,128)(2,1)S(1)}, bf16[3,4,128]{2,1,0:T(4,128)(2,1)}, u32[]{:S(2)}) copy-start(bf16[3,4,128]{2,1,0:T(4,128)(2,1)} %param.13) | copy-start | bytes 9220
  96.3 13.1 %copy-start.5 = (s32[3]{0:T(128)S(1)}, s32[3]{0:T(128)}, u32[]{:S(2)}) copy-start(s32[3]{0:T(128)} %param.16) | copy-start | bytes 40
  96.3 41.4 %all-to-all-start.1 = ((bf16[64,64,128]{2,1,0:T(8,128)(2,1)}), bf16[64,64,128]{2,1,0:T(8,128)(2,1)S(1)}, u32[]{:S(2)}, u32[]{:S(2)}) async-start(bf16[64,64,128]{2,1,0:T(8,128)(2,1)} %bitcast.10), calls=%async_computation.1 | async-start | bytes 2097152 | tf_op jit(solution)/shard_map/all_to_all | solution.py:314
